TPU v7x, 32 devices: a whole 2x2x4 slice. The times are simulated.
32 devices in a mesh: gx: 4 (over z), gy: 8 (over y, x, core).
Axes of the slice: x: 2, y: 2, z: 4, core: 2. Of those that a mesh axis runs over, the one named last changes fastest.
Arguments:
- conductivity: bfloat16 [2, 1024, 4096], P(None, 'gy', 'gx'), may hold values from 0.099609375 to 1.59375
Outputs:
- coarse_stencil: float32 [9, 8, 64, 2048], P(None, 'gy', 'gx')
All inputs are finite; a program needn't handle non-finite values.
Results may differ from a plain program's by a relative error of at most 0.0003.
Values may be sent and summed in bfloat16 or wider, within the bound.
A program may use at most 64 MiB of HBM per device.

v0:
```python
import functools

import jax
import jax.numpy as jnp
from jax import lax
from jax.experimental import pallas as pl
from jax.experimental.pallas import tpu as pltpu
from jax.sharding import PartitionSpec as P

MESH = pl.DeviceIdType.MESH
LANES = 128
UNROLL = 4
STEPS = 4
VMEM_LIMIT = 16 * 1024 * 1024


def arrivals(n, i):
    half = n // 2
    own_half = range(half) if i < half else range(half, n)
    if i < half:
        return [k for k in own_half if k != i] + list(range(n - 1, half - 1, -1))
    return [k for k in own_half if k < i] + list(range(half)) + [k for k in own_half if k > i]


def chosen(i, values):
    picked = values[-1]
    for at in range(len(values) - 2, -1, -1):
        picked = jnp.where(i == at, values[at], picked)
    return picked


def coarse_kernel(
    n, m, cells, fields, main, mid, tails, heads, south_in, north_in, pack,
    main_send, main_recv, mid_send, mid_recv, edge_send, edge_recv, known, own,
):
    i = lax.axis_index("gx")
    j = lax.axis_index("gy")
    band = main.shape[2]
    has_left, has_right = i > 0, i < n - 1
    has_south, has_north = j > 0, j < m - 1

    barrier = pltpu.get_barrier_semaphore()

    def greet(there, x, y):
        @pl.when(there)
        def _():
            pl.semaphore_signal(barrier, inc=1, device_id=(x, y), device_id_type=MESH)

    greet(has_left, i - 1, j)
    greet(has_right, i + 1, j)
    greet(has_south, i, j - 1)
    greet(has_north, i, j + 1)

    def rows_of(t):
        return cells.at[:, pl.ds(pl.multiple_of(t * band, band), band), :]

    loads = []
    for t in range(n):
        loads.append(pltpu.make_async_copy(cells.at[:, pl.ds(t * band + band - 8, 8), :], tails.at[t], own.at[2 * t]))
        loads.append(pltpu.make_async_copy(cells.at[:, pl.ds(t * band, 8), :], heads.at[t], own.at[2 * t + 1]))
    for load in loads:
        load.start()
    own_main = pltpu.make_async_copy(rows_of(i), main.at[i], own.at[2 * n])
    own_main.start()

    @pl.when(jnp.logical_not(has_south))
    def _():
        south_in[...] = jnp.ones(south_in.shape, south_in.dtype)

    @pl.when(jnp.logical_not(has_north))
    def _():
        north_in[...] = jnp.ones(north_in.shape, north_in.dtype)

    def one(there):
        return jnp.where(there, 1, 0)

    pl.semaphore_wait(barrier, one(has_left) + one(has_right) + one(has_south) + one(has_north))

    def tell(d):
        @pl.when(has_left & (i + d - 1 < n))
        def _():
            pl.semaphore_signal(known.at[0, d], inc=1, device_id=(i - 1, j), device_id_type=MESH)

        @pl.when(has_right & (i - d + 1 >= 0))
        def _():
            pl.semaphore_signal(known.at[1, d], inc=1, device_id=(i + 1, j), device_id_type=MESH)

    def hear(d):
        @pl.when(i + d < n)
        def _():
            pl.semaphore_wait(known.at[0, d], 1)

        @pl.when(i - d >= 0)
        def _():
            pl.semaphore_wait(known.at[1, d], 1)

    def remote(src, dst, send, recv, x, y):
        return pltpu.make_async_remote_copy(
            src_ref=src, dst_ref=dst, send_sem=send, recv_sem=recv, device_id=(x, y), device_id_type=MESH
        )

    def main_copy(t):
        return remote(rows_of(t), main.at[i], main_send.at[t], main_recv.at[i], t, j)

    def mid_copy(t):
        return remote(pack.at[t], mid.at[i], mid_send.at[t], mid_recv.at[i], t, j)

    def to_north():
        return remote(cells.at[:, pl.ds(n * band - 8, 8), :], south_in, edge_send.at[0], edge_recv.at[0], i, jnp.minimum(j + 1, m - 1))

    def to_south():
        return remote(cells.at[:, pl.ds(0, 8), :], north_in, edge_send.at[1], edge_recv.at[1], i, jnp.maximum(j - 1, 0))

    sub = lax.broadcasted_iota(jnp.int32, (8, cells.shape[2]), 0)

    def make_pack(t, under, over):
        low = [pltpu.roll(under[p].astype(jnp.float32), 2 + 2 * p, 0) for p in range(2)]
        high = [pltpu.roll(over[p].astype(jnp.float32), 4 + p, 0) for p in range(2)]
        rows = jnp.where(sub < 2, low[0], jnp.where(sub < 4, low[1], jnp.where(sub == 4, high[0], high[1])))
        pack[t] = rows.astype(jnp.bfloat16)

    def edges():
        @pl.when(has_south)
        def _():
            to_north().wait_recv()

        @pl.when(has_north)
        def _():
            to_south().wait_recv()

        make_pack(0, south_in, heads.at[1])
        make_pack(n - 1, tails.at[n - 2], north_in)

    tell(2)

    @pl.when(has_north)
    def _():
        to_north().start()

    @pl.when(has_south)
    def _():
        to_south().start()

    edge_phase = min(2, n - 1)
    for d in range(1, n):
        if d > 1:
            hear(d)
            if d < n - 1:
                tell(d + 1)

        @pl.when(i + d < n)
        def _():
            main_copy(i + d).start()

        @pl.when(i == d)
        def _():
            main_copy(0).start()

        if d == 1:
            for load in loads:
                load.wait()
            for t in range(1, n - 1):
                make_pack(t, tails.at[t - 1], heads.at[t + 1])

        @pl.when(i + d < n - 1)
        def _():
            mid_copy(i + d).start()

        if d == edge_phase:
            edges()

            @pl.when((i >= n - 1 - d) & has_right)
            def _():
                mid_copy(n - 1).start()

            @pl.when((i <= d) & has_left)
            def _():
                mid_copy(0).start()

        if d > edge_phase:
            @pl.when(i + d == n - 1)
            def _():
                mid_copy(n - 1).start()

        @pl.when(i == d)
        def _():
            if d > edge_phase:
                mid_copy(0).start()
            for t in range(1, d):
                main_copy(t).start()
                mid_copy(t).start()

    own_mid = pltpu.make_async_copy(pack.at[i], mid.at[i], own.at[2 * n + 1])
    own_mid.start()

    first = arrival_stage(n, m, main, mid, fields)
    own_main.wait()
    own_mid.wait()
    first(i)
    orders = [arrivals(n, at) for at in range(n)]
    for step in range(n - 1):
        k = chosen(i, [order[step] for order in orders])
        remote(pack.at[0], mid.at[k], mid_send.at[k], mid_recv.at[k], k, j).wait_recv()
        remote(rows_of(0), main.at[k], main_send.at[k], main_recv.at[k], k, j).wait_recv()
        first(k)

    for t in range(n):
        @pl.when(i != t)
        def _():
            main_copy(t).wait_send()
            mid_copy(t).wait_send()

    @pl.when(has_north)
    def _():
        to_north().wait_send()

    @pl.when(has_south)
    def _():
        to_south().wait_send()


def parts(x0, y0, x1, y1):
    s0, s1 = x0 + y0, x1 + y1
    return x0 * y0 * s1 + x1 * y1 * s0, s0 * s1


def two_faces(one, two):
    scale = 2.0 / (one[1] * two[1])
    return one[0] * two[1] * scale, two[0] * one[1] * scale


def middle(one, two):
    x, y = one[0] * two[1], two[0] * one[1]
    total = 1.0 / (x + y)
    return x * total, y * total, 2.0 * (one[0] * two[0]) * total


def verticals(pairs):
    sums = [x + y for x, y in pairs]
    low, high = sums[0] * sums[1], sums[2] * sums[3]
    scale = 4.0 / (low * high)
    low, high = high * scale, low * scale
    shares = (sums[1] * low, sums[0] * low, sums[3] * high, sums[2] * high)
    return [x * y * share for (x, y), share in zip(pairs, shares)]


def arrival_stage(n, m, main, mid, fields):
    band = main.shape[2]
    block = main.shape[3]
    half = band // 2
    rows = fields.shape[2]
    tiles = fields.shape[0] - 1
    per_block = block // (2 * LANES)
    i = lax.axis_index("gx")
    j = lax.axis_index("gy")
    last_rows = (i == n - 1) & (j == m - 1)

    taken = 2 * band + 8
    want = lax.broadcasted_iota(jnp.int32, (4 * rows, taken), 0)
    have = lax.broadcasted_iota(jnp.int32, (4 * rows, taken), 1)
    group = jnp.where(want >= 3 * rows, 3, jnp.where(want >= 2 * rows, 2, jnp.where(want >= rows, 1, 0)))
    place = want - group * rows
    plane = jnp.where(group >= 2, 1, 0)
    odd = group - 2 * plane
    inside = plane * band + 2 * jnp.where(place < half, place, 0) + odd
    above = jnp.where(odd == 0, 2 * band + 4 + plane, plane * band + 1)
    below = 2 * band + 2 * plane + odd
    source = jnp.where(place == half, above, jnp.where(place == rows - 1, below, inside))
    pick_rows = jnp.where(have == source, 1.0, 0.0).astype(jnp.bfloat16)
    fine = lax.broadcasted_iota(jnp.int32, (2 * LANES, 2 * LANES), 0)
    to = lax.broadcasted_iota(jnp.int32, (2 * LANES, 2 * LANES), 1)
    pick_cols = jnp.where(fine == jnp.where(to < LANES, 2 * to, 2 * (to - LANES) + 1), 1.0, 0.0).astype(jnp.bfloat16)

    top = (lax.broadcasted_iota(jnp.int32, (rows, LANES), 0) == half - 1) & last_rows

    def up(x):
        return pltpu.roll(x, rows - 1, 0)

    def tile_terms(k, part):
        t = k * per_block + part
        cols = pl.ds(pl.multiple_of(part * 2 * LANES, 2 * LANES), 2 * LANES)
        stored = jnp.concatenate(
            [
                main[k, 0, :, cols].astype(jnp.float32),
                main[k, 1, :, cols].astype(jnp.float32),
                mid[k, :, cols].astype(jnp.float32),
            ],
            axis=0,
        ).astype(jnp.bfloat16)
        picked = jnp.dot(pick_rows, stored, preferred_element_type=jnp.float32).astype(jnp.bfloat16)
        split = jnp.dot(picked, pick_cols, preferred_element_type=jnp.float32)
        a0, c0, a1, c1 = (split[g * rows : (g + 1) * rows, :LANES] for g in range(4))
        b0, d0, b1, d1 = (split[g * rows : (g + 1) * rows, LANES:] for g in range(4))
        def wall(x0, x1, inner):
            return jnp.where(top, 0.5 * (x0 + x1), inner[0]), jnp.where(top, 1.0, inner[1])

        s0, n0, t0 = middle(parts(a0, c0, a1, c1), wall(c0, c1, parts(c0, up(a0), c1, up(a1))))
        s1, n1, t1 = middle(parts(b0, d0, b1, d1), wall(d0, d1, parts(d0, up(b0), d1, up(b1))))
        h1, g1 = two_faces(parts(a0, b0, a1, b1), parts(c0, d0, c1, d1))
        pairs = ((a0, a1), (b0, b1), (c0, c1), (d0, d1))
        side_a, side_b, side_c, side_d = (
            (x + ((k0 + k1) + v)) - v for x, (k0, k1), v in zip((h1, h1, g1, g1), pairs, verticals(pairs))
        )
        for at, value in enumerate(
            (a0, a1, c0, c1, s0, n0, b0, b1, d0, d1, t0, s1, n1, t1, h1, g1, side_a, side_b, side_c, side_d)
        ):
            fields[t, at] = value

    def first(k):
        lax.fori_loop(0, per_block, lambda part, carry: (tile_terms(k, part), carry)[1], 0, unroll=UNROLL)

    ones = jnp.ones((rows, LANES), jnp.float32)
    for at in range(6):
        fields[tiles, at] = ones

    return first


def stencil_kernel(n, m, half, chunk, fields, out, held, sent):
    rows = fields.shape[2]
    tiles = fields.shape[0] - 1
    i = lax.axis_index("gx")
    j = lax.axis_index("gy")
    lane = lax.broadcasted_iota(jnp.int32, (rows, LANES), 1)
    sub = lax.broadcasted_iota(jnp.int32, (rows, LANES), 0)
    bottom = (sub == 0) & (i == 0) & (j == 0)
    top = (sub == half - 1) & (i == n - 1) & (j == m - 1)

    def up(x):
        return pltpu.roll(x, rows - 1, 0)

    def down(x):
        return pltpu.roll(x, 1, 0)

    def step(t, carry):
        last = (lane == LANES - 1) & (t == tiles - 1)
        first_lane = (lane == 0) & (t == 0)

        def ahead(at):
            return pltpu.roll(jnp.where(lane == 0, fields[t + 1, at], fields[t, at]), LANES - 1, 1)

        rolled = []

        def behind(x):
            turned = pltpu.roll(x, 1, 1)
            before = carry[len(rolled)]
            rolled.append(turned)
            return jnp.where(lane == 0, before, turned)

        a0, a1, c0, c1, s0, n0, b0, b1, d0, d1 = (fields[t, at] for at in range(10))
        t0, s1, n1, t1, h1, g1, side_a, side_b, side_c, side_d = (fields[t, at] for at in range(10, 20))
        wall_a, wall_b = a0 + a1, b0 + b1
        h2, g2 = two_faces(parts(b0, ahead(0), b1, ahead(1)), parts(d0, ahead(2), d1, ahead(3)))
        h2 = jnp.where(last, wall_b, h2)
        g2 = jnp.where(last, d0 + d1, g2)
        total = 1.0 / (h1 + h2)
        left, right = h1 * total, h2 * total
        left_up = up(left)
        right_up = up(right)
        s0_next = ahead(4)
        n0_next = ahead(5)
        side_a = side_a + jnp.where(first_lane, wall_a, behind(h2))
        side_c = side_c + jnp.where(first_lane, c0 + c1, behind(g2))
        side_b = side_b + h2
        side_d = side_d + g2

        nc = n0 * side_c
        sc = s0 * side_c
        nd = n1 * side_d
        sd = s1 * side_d
        even = side_a + t0 + s0 * sc + jnp.where(bottom, wall_a, down(t0 + n0 * nc))
        odd_ = side_b + t1 + s1 * sd + jnp.where(bottom, wall_b, down(t1 + n1 * nd))
        even_up = s0 * nc - t0
        odd_up = s1 * nd - t1
        sg = s0 * g1
        ng = n0 * g1
        sq = s0_next * g2
        nq = n0_next * g2
        p = h1 + s1 * sg + jnp.where(bottom, 0.0, down(n1 * ng))
        q = h2 + s1 * sq + jnp.where(bottom, 0.0, down(n1 * nq))
        p_up = n1 * sg
        p_down = s1 * ng
        q_up = s1 * nq
        q_down = n1 * sq

        mid = left * odd_ - p
        east = jnp.where(last, 0.0, right * mid - left * q)
        centre = even + left * (mid - p) + behind(right * (right * odd_ - 2.0 * q))
        lo = left * odd_up - p_up
        ro = right * odd_up - q_down
        north = even_up + left_up * lo - left * p_down + behind(right_up * ro - right * q_up)
        north = jnp.where(top, 0.0, north)
        north_east = jnp.where(last | top, 0.0, right_up * lo - left * q_up)
        north_west = jnp.where(last | top, 0.0, left_up * ro - right * p_down)
        west = behind(east)
        ne_back = behind(north_east)
        nw_back = behind(north_west)
        cols = pl.ds(pl.multiple_of(t * LANES, LANES), LANES)

        def below(x):
            return jnp.where(bottom, 0.0, down(x))

        for at, value in enumerate(
            (below(ne_back), below(north), below(north_west), west, centre, east, nw_back, north, north_east)
        ):
            held[at, :, cols] = value[:half]
        return tuple(rolled)

    def leave(c):
        cols = pl.ds(c * chunk * LANES, chunk * LANES)
        return pltpu.make_async_copy(held.at[:, :, cols], out.at[:, :, cols], sent.at[c])

    carry = (jnp.zeros((rows, LANES), jnp.float32),) * 7
    for c in range(tiles // chunk):
        carry = lax.fori_loop(c * chunk, (c + 1) * chunk, step, carry, unroll=STEPS)
        leave(c).start()
    for c in range(tiles // chunk):
        leave(c).wait()


def shards(n, m, conductivity):
    planes, local_rows, local_cols = conductivity.shape
    band = local_rows // n
    half = band // 2
    rows = -(-(half + 2) // 8) * 8
    tiles = n * local_cols // (2 * LANES)
    vmem = pl.BlockSpec(memory_space=pltpu.VMEM)
    anywhere = pl.BlockSpec(memory_space=pl.ANY)
    dma = pltpu.SemaphoreType.DMA
    shape = (tiles + 1, 20, rows, LANES)
    fields = pl.pallas_call(
        functools.partial(coarse_kernel, n, m),
        out_shape=jax.ShapeDtypeStruct(shape, jnp.float32),
        in_specs=[anywhere],
        out_specs=vmem,
        scratch_shapes=[
            pltpu.VMEM((n, planes, band, local_cols), jnp.bfloat16),
            pltpu.VMEM((n, 8, local_cols), jnp.bfloat16),
            pltpu.VMEM((n, planes, 8, local_cols), jnp.bfloat16),
            pltpu.VMEM((n, planes, 8, local_cols), jnp.bfloat16),
            pltpu.VMEM((planes, 8, local_cols), jnp.bfloat16),
            pltpu.VMEM((planes, 8, local_cols), jnp.bfloat16),
            pltpu.VMEM((n, 8, local_cols), jnp.bfloat16),
            dma((n,)),
            dma((n,)),
            dma((n,)),
            dma((n,)),
            dma((2,)),
            dma((2,)),
            pltpu.SemaphoreType.REGULAR((2, n)),
            dma((2 * n + 2,)),
        ],
        compiler_params=pltpu.CompilerParams(
            collective_id=0, has_side_effects=True, vmem_limit_bytes=VMEM_LIMIT
        ),
        name="coarse",
    )(pltpu.with_memory_space_constraint(conductivity, pltpu.HBM))
    chunk = tiles // 4
    stencil = pl.pallas_call(
        functools.partial(stencil_kernel, n, m, half, chunk),
        out_shape=jax.ShapeDtypeStruct((9, half, tiles * LANES), jnp.float32),
        in_specs=[vmem],
        out_specs=anywhere,
        scratch_shapes=[pltpu.VMEM((9, half, tiles * LANES), jnp.float32), dma((4,))],
        compiler_params=pltpu.CompilerParams(vmem_limit_bytes=VMEM_LIMIT),
        name="stencil",
    )(fields)
    return stencil[:, None]


def solution(mesh):
    n, m = mesh.shape["gx"], mesh.shape["gy"]
    return jax.shard_map(
        functools.partial(shards, n, m),
        mesh=mesh,
        in_specs=(P(None, "gy", "gx"),),
        out_specs=P(None, "gy", "gx", None),
        check_vma=False,
    )
```

profile of v0, /device:TPU:13, one launch (start us, length us, event | category | flops | bytes accessed | tf_op | source)
XLA Modules:
  0.0 20.9 jit_solution(10404644696264540155)
XLA Ops:
  0.0 18.5 %coarse.1.fields = f32[17,20,24,128]{3,2,1,0:T(8,128)S(1)} custom-call(bf16[2,128,1024]{2,1,0:T(8,128)(2,1)} %cells.1), custom_call_target="tpu_custom_call" | custom-call | tf_op jit(solution)/shard_map/coarse/pallas_call | solution.py:431
  18.5 2.4 %stencil.1 = f32[9,16,2048]{2,1,0:T(8,128)} custom-call(f32[17,20,24,128]{3,2,1,0:T(8,128)S(1)} %coarse.1.fields), custom_call_target="tpu_custom_call" | custom-call | tf_op jit(solution)/shard_map/stencil/pallas_call | solution.py:459
where the time goes:
time: 21.1 us; the launch traced here: 20.9 us
  Pallas kernels  20.9 us (99%)
    pallas_call x1, Pallas kernels, shards(): pl.pallas_call(functools.partial(coarse_kernel, n, m), out_shape=jax.Shap...  18.5 us
    pallas_call x1, Pallas kernels, shards(): pl.pallas_call(functools.partial(stencil_kernel, n, m, half, chunk), out_...  2.41 us

commit v1 on v0

--- a/solution.py
+++ b/solution.py
@@ -38,18 +38,26 @@
     band = main.shape[2]
     has_left, has_right = i > 0, i < n - 1
     has_south, has_north = j > 0, j < m - 1
+    before, after = jnp.maximum(j - 1, 0), jnp.minimum(j + 1, m - 1)
+
+    def signal(sem, x, y):
+        pl.semaphore_signal(sem, inc=1, device_id=(x, y), device_id_type=MESH)
 
     barrier = pltpu.get_barrier_semaphore()
-
-    def greet(there, x, y):
-        @pl.when(there)
+    for t in range(1, n):
+        @pl.when(i < t)
         def _():
-            pl.semaphore_signal(barrier, inc=1, device_id=(x, y), device_id_type=MESH)
-
-    greet(has_left, i - 1, j)
-    greet(has_right, i + 1, j)
-    greet(has_south, i, j - 1)
-    greet(has_north, i, j + 1)
+            signal(barrier, t, j)
+
+    @pl.when(has_north)
+    def _():
+        signal(barrier, i, after)
+
+    first_of_all = (i == 0) & (j == 0)
+
+    @pl.when((i == 0) & (j == 1))
+    def _():
+        signal(barrier, 0, 0)
 
     def rows_of(t):
         return cells.at[:, pl.ds(pl.multiple_of(t * band, band), band), :]
@@ -71,29 +79,6 @@
     def _():
         north_in[...] = jnp.ones(north_in.shape, north_in.dtype)
 
-    def one(there):
-        return jnp.where(there, 1, 0)
-
-    pl.semaphore_wait(barrier, one(has_left) + one(has_right) + one(has_south) + one(has_north))
-
-    def tell(d):
-        @pl.when(has_left & (i + d - 1 < n))
-        def _():
-            pl.semaphore_signal(known.at[0, d], inc=1, device_id=(i - 1, j), device_id_type=MESH)
-
-        @pl.when(has_right & (i - d + 1 >= 0))
-        def _():
-            pl.semaphore_signal(known.at[1, d], inc=1, device_id=(i + 1, j), device_id_type=MESH)
-
-    def hear(d):
-        @pl.when(i + d < n)
-        def _():
-            pl.semaphore_wait(known.at[0, d], 1)
-
-        @pl.when(i - d >= 0)
-        def _():
-            pl.semaphore_wait(known.at[1, d], 1)
-
     def remote(src, dst, send, recv, x, y):
         return pltpu.make_async_remote_copy(
             src_ref=src, dst_ref=dst, send_sem=send, recv_sem=recv, device_id=(x, y), device_id_type=MESH
@@ -106,10 +91,10 @@
         return remote(pack.at[t], mid.at[i], mid_send.at[t], mid_recv.at[i], t, j)
 
     def to_north():
-        return remote(cells.at[:, pl.ds(n * band - 8, 8), :], south_in, edge_send.at[0], edge_recv.at[0], i, jnp.minimum(j + 1, m - 1))
+        return remote(cells.at[:, pl.ds(n * band - 8, 8), :], south_in, edge_send.at[0], edge_recv.at[0], i, after)
 
     def to_south():
-        return remote(cells.at[:, pl.ds(0, 8), :], north_in, edge_send.at[1], edge_recv.at[1], i, jnp.maximum(j - 1, 0))
+        return remote(cells.at[:, pl.ds(0, 8), :], north_in, edge_send.at[1], edge_recv.at[1], i, before)
 
     sub = lax.broadcasted_iota(jnp.int32, (8, cells.shape[2]), 0)
 
@@ -119,76 +104,72 @@
         rows = jnp.where(sub < 2, low[0], jnp.where(sub < 4, low[1], jnp.where(sub == 4, high[0], high[1])))
         pack[t] = rows.astype(jnp.bfloat16)
 
-    def edges():
-        @pl.when(has_south)
+    pl.semaphore_wait(barrier, i + jnp.where(has_south | first_of_all, 1, 0))
+
+    @pl.when(has_left)
+    def _():
+        main_copy(0).start()
+
+    for t in range(n - 2, -1, -1):
+        @pl.when(i > t)
         def _():
-            to_north().wait_recv()
-
-        @pl.when(has_north)
+            signal(known.at[i], t, j)
+
+    @pl.when(has_south)
+    def _():
+        signal(known.at[0], i, before)
+        to_south().start()
+
+    for load in loads:
+        load.wait()
+    for t in range(1, n - 1):
+        make_pack(t, tails.at[t - 1], heads.at[t + 1])
+
+    @pl.when(has_right)
+    def _():
+        pl.semaphore_wait(known.at[i + 1], 1)
+        main_copy(i + 1).start()
+
+    @pl.when(i + 1 < n - 1)
+    def _():
+        mid_copy(i + 1).start()
+
+    @pl.when(has_north)
+    def _():
+        pl.semaphore_wait(known.at[0], 1)
+        to_north().start()
+
+    @pl.when(has_south)
+    def _():
+        to_north().wait_recv()
+
+    @pl.when(has_north)
+    def _():
+        to_south().wait_recv()
+
+    make_pack(0, south_in, heads.at[1])
+    make_pack(n - 1, tails.at[n - 2], north_in)
+
+    @pl.when(i + 1 == n - 1)
+    def _():
+        mid_copy(n - 1).start()
+
+    @pl.when(has_left)
+    def _():
+        mid_copy(0).start()
+
+    for t in range(1, n - 1):
+        @pl.when(i > t)
         def _():
-            to_south().wait_recv()
-
-        make_pack(0, south_in, heads.at[1])
-        make_pack(n - 1, tails.at[n - 2], north_in)
-
-    tell(2)
-
-    @pl.when(has_north)
-    def _():
-        to_north().start()
-
-    @pl.when(has_south)
-    def _():
-        to_south().start()
-
-    edge_phase = min(2, n - 1)
-    for d in range(1, n):
-        if d > 1:
-            hear(d)
-            if d < n - 1:
-                tell(d + 1)
-
-        @pl.when(i + d < n)
+            main_copy(t).start()
+            mid_copy(t).start()
+
+    for t in range(2, n):
+        @pl.when(i + 1 < t)
         def _():
-            main_copy(i + d).start()
-
-        @pl.when(i == d)
-        def _():
-            main_copy(0).start()
-
-        if d == 1:
-            for load in loads:
-                load.wait()
-            for t in range(1, n - 1):
-                make_pack(t, tails.at[t - 1], heads.at[t + 1])
-
-        @pl.when(i + d < n - 1)
-        def _():
-            mid_copy(i + d).start()
-
-        if d == edge_phase:
-            edges()
-
-            @pl.when((i >= n - 1 - d) & has_right)
-            def _():
-                mid_copy(n - 1).start()
-
-            @pl.when((i <= d) & has_left)
-            def _():
-                mid_copy(0).start()
-
-        if d > edge_phase:
-            @pl.when(i + d == n - 1)
-            def _():
-                mid_copy(n - 1).start()
-
-        @pl.when(i == d)
-        def _():
-            if d > edge_phase:
-                mid_copy(0).start()
-            for t in range(1, d):
-                main_copy(t).start()
-                mid_copy(t).start()
+            pl.semaphore_wait(known.at[t], 1)
+            main_copy(t).start()
+            mid_copy(t).start()
 
     own_mid = pltpu.make_async_copy(pack.at[i], mid.at[i], own.at[2 * n + 1])
     own_mid.start()
@@ -447,7 +428,7 @@
             dma((n,)),
             dma((2,)),
             dma((2,)),
-            pltpu.SemaphoreType.REGULAR((2, n)),
+            pltpu.SemaphoreType.REGULAR((n,)),
             dma((2 * n + 2,)),
         ],
         compiler_params=pltpu.CompilerParams(

time: 21.1 us -> 19.3 us (0.915)
  the two profiles are of different devices: /device:TPU:13 before, /device:TPU:0 now
where the time goes in v1:
time: 19.3 us; the launch traced here: 19.1 us
  Pallas kernels  19.1 us (99%)
    pallas_call x1, Pallas kernels, shards(): pl.pallas_call(functools.partial(coarse_kernel, n, m), out_shape=jax.Shap...  16.7 us
    pallas_call x1, Pallas kernels, shards(): pl.pallas_call(functools.partial(stencil_kernel, n, m, half, chunk), out_...  2.41 us

profile of v1, /device:TPU:0, one launch (start us, length us, event | category | flops | bytes accessed | tf_op | source)
XLA Modules:
  0.0 19.1 jit_solution(758325316759422496)
XLA Ops:
  0.0 16.7 %coarse.1.fields = f32[17,20,24,128]{3,2,1,0:T(8,128)S(1)} custom-call(bf16[2,128,1024]{2,1,0:T(8,128)(2,1)} %cells.1), custom_call_target="tpu_custom_call" | custom-call | tf_op jit(solution)/shard_map/coarse/pallas_call | solution.py:412
  16.7 2.4 %stencil.1 = f32[9,16,2048]{2,1,0:T(8,128)} custom-call(f32[17,20,24,128]{3,2,1,0:T(8,128)S(1)} %coarse.1.fields), custom_call_target="tpu_custom_call" | custom-call | tf_op jit(solution)/shard_map/stencil/pallas_call | solution.py:440

commit v2 on v1

--- a/solution.py
+++ b/solution.py
@@ -10,7 +10,6 @@
 MESH = pl.DeviceIdType.MESH
 LANES = 128
 UNROLL = 4
-STEPS = 4
 VMEM_LIMIT = 16 * 1024 * 1024
 
 
@@ -22,6 +21,25 @@
     return [k for k in own_half if k < i] + list(range(half)) + [k for k in own_half if k > i]
 
 
+def spans(n, i, per_block):
+    tiles = n * per_block
+    there, found = set(), []
+    for k in [i] + arrivals(n, i):
+        new = set(range(k * per_block, (k + 1) * per_block))
+        there |= new
+        ready = [
+            t for t in range(tiles)
+            if {max(t - 1, 0), t, min(t + 1, tiles - 1)} <= there and {t - 1, t, t + 1} & new
+        ]
+        found.append((ready[0], ready[-1] + 1) if ready else (0, 0))
+    return found
+
+
+def last_span(n, i, per_block):
+    first, end = spans(n, i, per_block)[-1]
+    return min(first, n * per_block - per_block - 2)
+
+
 def chosen(i, values):
     picked = values[-1]
     for at in range(len(values) - 2, -1, -1):
@@ -30,7 +48,7 @@
 
 
 def coarse_kernel(
-    n, m, cells, fields, main, mid, tails, heads, south_in, north_in, pack,
+    n, m, cells, fields, held, main, mid, tails, heads, south_in, north_in, pack,
     main_send, main_recv, mid_send, mid_recv, edge_send, edge_recv, known, own,
 ):
     i = lax.axis_index("gx")
@@ -175,15 +193,34 @@
     own_mid.start()
 
     first = arrival_stage(n, m, main, mid, fields)
+    tile_stencil, carry_into = stencil_stage(n, m, band // 2, fields)
+    per_block = cells.shape[2] // (2 * LANES)
+    ranges = [spans(n, at, per_block) for at in range(n)]
+
+    def second(step):
+        low, end = (chosen(i, [found[step][side] for found in ranges]) for side in range(2))
+
+        def one(t, carry):
+            values, carry = tile_stencil(t, carry)
+            cols = pl.ds(pl.multiple_of(t * LANES, LANES), LANES)
+            for at, value in enumerate(values):
+                held[at, :, cols] = value
+            return carry
+
+        lax.fori_loop(low, end, one, carry_into(low))
+
     own_main.wait()
     own_mid.wait()
     first(i)
+    second(0)
     orders = [arrivals(n, at) for at in range(n)]
     for step in range(n - 1):
         k = chosen(i, [order[step] for order in orders])
         remote(pack.at[0], mid.at[k], mid_send.at[k], mid_recv.at[k], k, j).wait_recv()
         remote(rows_of(0), main.at[k], main_send.at[k], main_recv.at[k], k, j).wait_recv()
         first(k)
+        if step < n - 2:
+            second(step + 1)
 
     for t in range(n):
         @pl.when(i != t)
@@ -297,7 +334,7 @@
     return first
 
 
-def stencil_kernel(n, m, half, chunk, fields, out, held, sent):
+def stencil_stage(n, m, half, fields):
     rows = fields.shape[2]
     tiles = fields.shape[0] - 1
     i = lax.axis_index("gx")
@@ -376,26 +413,53 @@
         west = behind(east)
         ne_back = behind(north_east)
         nw_back = behind(north_west)
-        cols = pl.ds(pl.multiple_of(t * LANES, LANES), LANES)
 
         def below(x):
             return jnp.where(bottom, 0.0, down(x))
 
-        for at, value in enumerate(
-            (below(ne_back), below(north), below(north_west), west, centre, east, nw_back, north, north_east)
-        ):
-            held[at, :, cols] = value[:half]
-        return tuple(rolled)
+        values = (below(ne_back), below(north), below(north_west), west, centre, east, nw_back, north, north_east)
+        return tuple(value[:half] for value in values), tuple(rolled)
+
+    def carry_into(t):
+        carry = step(jnp.maximum(t - 1, 0), (jnp.zeros((rows, LANES), jnp.float32),) * 7)[1]
+        return tuple(jnp.where(t > 0, x, 0.0) for x in carry)
+
+    return step, carry_into
+
+
+def stencil_kernel(n, m, half, per_block, fields, held, out, late, sent):
+    tiles = fields.shape[0] - 1
+    count = per_block + 2
+    i = lax.axis_index("gx")
+    low = chosen(i, [last_span(n, at, per_block) for at in range(n)])
+    tile_stencil, carry_into = stencil_stage(n, m, half, fields)
+
+    def columns(t, width):
+        return pl.ds(pl.multiple_of(t * LANES, LANES), width * LANES)
+
+    def early(q):
+        cols = columns(jnp.where(q < low, q, q + count), 1)
+        return pltpu.make_async_copy(held.at[:, :, cols], out.at[:, :, cols], sent.at[q])
+
+    for q in range(tiles - count):
+        early(q).start()
 
     def leave(c):
-        cols = pl.ds(c * chunk * LANES, chunk * LANES)
-        return pltpu.make_async_copy(held.at[:, :, cols], out.at[:, :, cols], sent.at[c])
-
-    carry = (jnp.zeros((rows, LANES), jnp.float32),) * 7
-    for c in range(tiles // chunk):
-        carry = lax.fori_loop(c * chunk, (c + 1) * chunk, step, carry, unroll=STEPS)
-        leave(c).start()
-    for c in range(tiles // chunk):
+        return pltpu.make_async_copy(
+            late.at[:, :, pl.ds(c * 2 * LANES, 2 * LANES)], out.at[:, :, columns(low + 2 * c, 2)],
+            sent.at[tiles - count + c],
+        )
+
+    carry = carry_into(low)
+    for q in range(count):
+        values, carry = tile_stencil(low + q, carry)
+        for at, value in enumerate(values):
+            late[at, :, q * LANES : (q + 1) * LANES] = value
+        if q % 2:
+            leave(q // 2).start()
+    for q in range(tiles - count):
+        early(q).wait()
+    for c in range(count // 2):
         leave(c).wait()
 
 
@@ -409,11 +473,13 @@
     anywhere = pl.BlockSpec(memory_space=pl.ANY)
     dma = pltpu.SemaphoreType.DMA
     shape = (tiles + 1, 20, rows, LANES)
-    fields = pl.pallas_call(
+    per_block = local_cols // (2 * LANES)
+    result = jax.ShapeDtypeStruct((9, half, tiles * LANES), jnp.float32)
+    fields, held = pl.pallas_call(
         functools.partial(coarse_kernel, n, m),
-        out_shape=jax.ShapeDtypeStruct(shape, jnp.float32),
+        out_shape=(jax.ShapeDtypeStruct(shape, jnp.float32), result),
         in_specs=[anywhere],
-        out_specs=vmem,
+        out_specs=(vmem, vmem),
         scratch_shapes=[
             pltpu.VMEM((n, planes, band, local_cols), jnp.bfloat16),
             pltpu.VMEM((n, 8, local_cols), jnp.bfloat16),
@@ -436,16 +502,16 @@
         ),
         name="coarse",
     )(pltpu.with_memory_space_constraint(conductivity, pltpu.HBM))
-    chunk = tiles // 4
+    count = per_block + 2
     stencil = pl.pallas_call(
-        functools.partial(stencil_kernel, n, m, half, chunk),
-        out_shape=jax.ShapeDtypeStruct((9, half, tiles * LANES), jnp.float32),
-        in_specs=[vmem],
+        functools.partial(stencil_kernel, n, m, half, per_block),
+        out_shape=result,
+        in_specs=[vmem, vmem],
         out_specs=anywhere,
-        scratch_shapes=[pltpu.VMEM((9, half, tiles * LANES), jnp.float32), dma((4,))],
+        scratch_shapes=[pltpu.VMEM((9, half, count * LANES), jnp.float32), dma((tiles - count + count // 2,))],
         compiler_params=pltpu.CompilerParams(vmem_limit_bytes=VMEM_LIMIT),
         name="stencil",
-    )(fields)
+    )(fields, held)
     return stencil[:, None]
 
 

time: 19.3 us -> 18.3 us (0.948)
  Pallas kernels: 19.1 us -> 18.1 us
    pallas_call x2, Pallas kernels: 19.1 us -> 18.1 us  [the longest x1 16.7 us: shards(): pl.pallas_call(functools.partial(coarse_kernel, n, m), out_shape=(jax.Sha...]
where the time goes in v2:
time: 18.3 us; the launch traced here: 18.1 us
  Pallas kernels  18.1 us (99%)
    pallas_call x1, Pallas kernels, shards(): pl.pallas_call(functools.partial(coarse_kernel, n, m), out_shape=(jax.Sha...  16.7 us
    pallas_call x1, Pallas kernels, shards(): pl.pallas_call(functools.partial(stencil_kernel, n, m, half, per_block),...  1.4 us

profile of v2, /device:TPU:0, one launch (start us, length us, event | category | flops | bytes accessed | tf_op | source)
XLA Modules:
  0.0 18.1 jit_solution(10051417696983325505)
XLA Ops:
  0.0 16.7 %coarse.1 = (f32[17,20,24,128]{3,2,1,0:T(8,128)S(1)}, f32[9,16,2048]{2,1,0:T(8,128)S(1)}) custom-call(bf16[2,128,1024]{2,1,0:T(8,128)(2,1)} %cells.1), custom_call_target="tpu_custom_call" | custom-call | tf_op jit(solution)/shard_map/coarse/pallas_call | solution.py:478
  16.7 1.4 %stencil.1 = f32[9,16,2048]{2,1,0:T(8,128)} custom-call(f32[17,20,24,128]{3,2,1,0:T(8,128)S(1)} %get-tuple-element.7.fields, f32[9,16,2048]{2,1,0:T(8,128)S(1)} %get-tuple-element.8.held), custom_call_target="tpu_custom_call" | custom-call | tf_op jit(solution)/shard_map/stencil/pallas_call | solution.py:506

commit v3 on v2

--- a/solution.py
+++ b/solution.py
@@ -9,23 +9,25 @@
 
 MESH = pl.DeviceIdType.MESH
 LANES = 128
-UNROLL = 4
+PIECES = 2
 VMEM_LIMIT = 16 * 1024 * 1024
 
 
 def arrivals(n, i):
     half = n // 2
-    own_half = range(half) if i < half else range(half, n)
     if i < half:
-        return [k for k in own_half if k != i] + list(range(n - 1, half - 1, -1))
-    return [k for k in own_half if k < i] + list(range(half)) + [k for k in own_half if k > i]
+        return list(range(i)) + list(range(n - 1, half, -1)) + list(range(i + 1, half)) + [half]
+    return list(range(half, i)) + list(range(half - 1)) + list(range(i + 1, n)) + [half - 1]
 
 
 def spans(n, i, per_block):
-    tiles = n * per_block
+    tiles, piece = n * per_block, per_block // PIECES
+    order = [i] + arrivals(n, i)
+    arrived = [set(range(k * per_block, (k + 1) * per_block)) for k in order[:-1]]
+    last = order[-1] * per_block
+    arrived += [set(range(last + p * piece, last + (p + 1) * piece)) for p in range(PIECES)]
     there, found = set(), []
-    for k in [i] + arrivals(n, i):
-        new = set(range(k * per_block, (k + 1) * per_block))
+    for new in arrived:
         there |= new
         ready = [
             t for t in range(tiles)
@@ -35,9 +37,12 @@
     return found
 
 
-def last_span(n, i, per_block):
-    first, end = spans(n, i, per_block)[-1]
-    return min(first, n * per_block - per_block - 2)
+def last_count(per_block):
+    return per_block // PIECES + 2
+
+
+def last_low(n, i, per_block):
+    return min(spans(n, i, per_block)[-1][0], n * per_block - last_count(per_block))
 
 
 def chosen(i, values):
@@ -48,12 +53,14 @@
 
 
 def coarse_kernel(
-    n, m, cells, fields, held, main, mid, tails, heads, south_in, north_in, pack,
-    main_send, main_recv, mid_send, mid_recv, edge_send, edge_recv, known, own,
+    n, m, cells, fields, held, carried, blocks, rims, south_in, north_in, pack,
+    arrived, sent, edge_sent, edge_arrived, known, own,
 ):
     i = lax.axis_index("gx")
     j = lax.axis_index("gy")
-    band = main.shape[2]
+    block = cells.shape[2]
+    band = cells.shape[1] // n
+    width = block // PIECES
     has_left, has_right = i > 0, i < n - 1
     has_south, has_north = j > 0, j < m - 1
     before, after = jnp.maximum(j - 1, 0), jnp.minimum(j + 1, m - 1)
@@ -78,16 +85,16 @@
         signal(barrier, 0, 0)
 
     def rows_of(t):
-        return cells.at[:, pl.ds(pl.multiple_of(t * band, band), band), :]
+        return pl.ds(pl.multiple_of(t * band, band), band)
 
     loads = []
-    for t in range(n):
-        loads.append(pltpu.make_async_copy(cells.at[:, pl.ds(t * band + band - 8, 8), :], tails.at[t], own.at[2 * t]))
-        loads.append(pltpu.make_async_copy(cells.at[:, pl.ds(t * band, 8), :], heads.at[t], own.at[2 * t + 1]))
+    for t in range(n - 1):
+        loads.append(pltpu.make_async_copy(cells.at[:, pl.ds((t + 1) * band - 8, 8), :], rims.at[0, t], own.at[0]))
+        loads.append(pltpu.make_async_copy(cells.at[:, pl.ds((t + 1) * band, 8), :], rims.at[1, t], own.at[0]))
+    for plane in range(2):
+        loads.append(pltpu.make_async_copy(cells.at[plane, rows_of(i), :], blocks.at[i, pl.ds(plane * band, band), :], own.at[1]))
     for load in loads:
         load.start()
-    own_main = pltpu.make_async_copy(rows_of(i), main.at[i], own.at[2 * n])
-    own_main.start()
 
     @pl.when(jnp.logical_not(has_south))
     def _():
@@ -102,19 +109,35 @@
             src_ref=src, dst_ref=dst, send_sem=send, recv_sem=recv, device_id=(x, y), device_id_type=MESH
         )
 
-    def main_copy(t):
-        return remote(rows_of(t), main.at[i], main_send.at[t], main_recv.at[i], t, j)
-
-    def mid_copy(t):
-        return remote(pack.at[t], mid.at[i], mid_send.at[t], mid_recv.at[i], t, j)
+    def cols_of(p):
+        return pl.ds(p * width, width)
+
+    def send_rows(t, p):
+        for plane in range(2):
+            remote(
+                cells.at[plane, rows_of(t), cols_of(p)], blocks.at[i, pl.ds(plane * band, band), cols_of(p)],
+                sent.at[0], arrived.at[i, p], t, j,
+            ).start()
+
+    def send_halo(t, p):
+        remote(
+            pack.at[t, :, cols_of(p)], blocks.at[i, pl.ds(2 * band, 8), cols_of(p)], sent.at[0], arrived.at[i, p], t, j
+        ).start()
+
+    def send(t, rows, halo):
+        for p in range(PIECES):
+            if halo:
+                send_halo(t, p)
+            if rows:
+                send_rows(t, p)
 
     def to_north():
-        return remote(cells.at[:, pl.ds(n * band - 8, 8), :], south_in, edge_send.at[0], edge_recv.at[0], i, after)
+        return remote(cells.at[:, pl.ds(n * band - 8, 8), :], south_in, edge_sent.at[0], edge_arrived.at[0], i, after)
 
     def to_south():
-        return remote(cells.at[:, pl.ds(0, 8), :], north_in, edge_send.at[1], edge_recv.at[1], i, before)
-
-    sub = lax.broadcasted_iota(jnp.int32, (8, cells.shape[2]), 0)
+        return remote(cells.at[:, pl.ds(0, 8), :], north_in, edge_sent.at[1], edge_arrived.at[1], i, before)
+
+    sub = lax.broadcasted_iota(jnp.int32, (8, block), 0)
 
     def make_pack(t, under, over):
         low = [pltpu.roll(under[p].astype(jnp.float32), 2 + 2 * p, 0) for p in range(2)]
@@ -126,7 +149,7 @@
 
     @pl.when(has_left)
     def _():
-        main_copy(0).start()
+        send(0, True, False)
 
     for t in range(n - 2, -1, -1):
         @pl.when(i > t)
@@ -138,19 +161,18 @@
         signal(known.at[0], i, before)
         to_south().start()
 
-    for load in loads:
-        load.wait()
+    pltpu.make_async_copy(rims, rims, own.at[0]).wait()
     for t in range(1, n - 1):
-        make_pack(t, tails.at[t - 1], heads.at[t + 1])
+        make_pack(t, rims.at[0, t - 1], rims.at[1, t])
 
     @pl.when(has_right)
     def _():
         pl.semaphore_wait(known.at[i + 1], 1)
-        main_copy(i + 1).start()
+        send(i + 1, True, False)
 
     @pl.when(i + 1 < n - 1)
     def _():
-        mid_copy(i + 1).start()
+        send(i + 1, False, True)
 
     @pl.when(has_north)
     def _():
@@ -165,36 +187,34 @@
     def _():
         to_south().wait_recv()
 
-    make_pack(0, south_in, heads.at[1])
-    make_pack(n - 1, tails.at[n - 2], north_in)
+    make_pack(0, south_in, rims.at[1, 0])
+    make_pack(n - 1, rims.at[0, n - 2], north_in)
 
     @pl.when(i + 1 == n - 1)
     def _():
-        mid_copy(n - 1).start()
+        send(n - 1, False, True)
 
     @pl.when(has_left)
     def _():
-        mid_copy(0).start()
+        send(0, False, True)
 
     for t in range(1, n - 1):
         @pl.when(i > t)
         def _():
-            main_copy(t).start()
-            mid_copy(t).start()
+            send(t, True, True)
 
     for t in range(2, n):
         @pl.when(i + 1 < t)
         def _():
             pl.semaphore_wait(known.at[t], 1)
-            main_copy(t).start()
-            mid_copy(t).start()
-
-    own_mid = pltpu.make_async_copy(pack.at[i], mid.at[i], own.at[2 * n + 1])
-    own_mid.start()
-
-    first = arrival_stage(n, m, main, mid, fields)
+            send(t, True, True)
+
+    blocks[i, pl.ds(2 * band, 8), :] = pack[i]
+
+    first = arrival_stage(n, m, band, blocks, fields)
     tile_stencil, carry_into = stencil_stage(n, m, band // 2, fields)
-    per_block = cells.shape[2] // (2 * LANES)
+    per_block = block // (2 * LANES)
+    per_piece = per_block // PIECES
     ranges = [spans(n, at, per_block) for at in range(n)]
 
     def second(step):
@@ -209,24 +229,34 @@
 
         lax.fori_loop(low, end, one, carry_into(low))
 
-    own_main.wait()
-    own_mid.wait()
-    first(i)
+    def await_piece(k, p):
+        landed = blocks.at[k, :, cols_of(p)]
+        remote(landed, landed, sent.at[0], arrived.at[k, p], k, j).wait_recv()
+
+    mine = blocks.at[i, pl.ds(0, 2 * band), :]
+    pltpu.make_async_copy(mine, mine, own.at[1]).wait()
+    first(i, 0, per_block)
     second(0)
     orders = [arrivals(n, at) for at in range(n)]
-    for step in range(n - 1):
+    for step in range(n - 2):
         k = chosen(i, [order[step] for order in orders])
-        remote(pack.at[0], mid.at[k], mid_send.at[k], mid_recv.at[k], k, j).wait_recv()
-        remote(rows_of(0), main.at[k], main_send.at[k], main_recv.at[k], k, j).wait_recv()
-        first(k)
-        if step < n - 2:
-            second(step + 1)
-
-    for t in range(n):
-        @pl.when(i != t)
-        def _():
-            main_copy(t).wait_send()
-            mid_copy(t).wait_send()
+        for p in range(PIECES):
+            await_piece(k, p)
+        first(k, 0, per_block)
+        second(step + 1)
+    k = chosen(i, [order[n - 2] for order in orders])
+    for p in range(PIECES):
+        if p == PIECES - 1:
+            low = chosen(i, [last_low(n, at, per_block) for at in range(n)])
+            for at, value in enumerate(carry_into(low)):
+                carried[at] = value
+        await_piece(k, p)
+        first(k, p * per_piece, per_piece)
+        if p < PIECES - 1:
+            second(n - 1 + p)
+
+    others = blocks.at[pl.ds(0, n - 1)]
+    remote(others, others, sent.at[0], arrived.at[0, 0], i, j).wait_send()
 
     @pl.when(has_north)
     def _():
@@ -262,9 +292,8 @@
     return [x * y * share for (x, y), share in zip(pairs, shares)]
 
 
-def arrival_stage(n, m, main, mid, fields):
-    band = main.shape[2]
-    block = main.shape[3]
+def arrival_stage(n, m, band, blocks, fields):
+    block = blocks.shape[2]
     half = band // 2
     rows = fields.shape[2]
     tiles = fields.shape[0] - 1
@@ -296,15 +325,8 @@
 
     def tile_terms(k, part):
         t = k * per_block + part
-        cols = pl.ds(pl.multiple_of(part * 2 * LANES, 2 * LANES), 2 * LANES)
-        stored = jnp.concatenate(
-            [
-                main[k, 0, :, cols].astype(jnp.float32),
-                main[k, 1, :, cols].astype(jnp.float32),
-                mid[k, :, cols].astype(jnp.float32),
-            ],
-            axis=0,
-        ).astype(jnp.bfloat16)
+        cols = pl.ds(part * 2 * LANES, 2 * LANES)
+        stored = blocks[k, :, cols]
         picked = jnp.dot(pick_rows, stored, preferred_element_type=jnp.float32).astype(jnp.bfloat16)
         split = jnp.dot(picked, pick_cols, preferred_element_type=jnp.float32)
         a0, c0, a1, c1 = (split[g * rows : (g + 1) * rows, :LANES] for g in range(4))
@@ -324,8 +346,9 @@
         ):
             fields[t, at] = value
 
-    def first(k):
-        lax.fori_loop(0, per_block, lambda part, carry: (tile_terms(k, part), carry)[1], 0, unroll=UNROLL)
+    def first(k, start, count):
+        for part in range(start, start + count):
+            tile_terms(k, part)
 
     ones = jnp.ones((rows, LANES), jnp.float32)
     for at in range(6):
@@ -427,40 +450,27 @@
     return step, carry_into
 
 
-def stencil_kernel(n, m, half, per_block, fields, held, out, late, sent):
+def stencil_kernel(n, m, half, per_block, fields, held, carried, out, late, stored):
     tiles = fields.shape[0] - 1
-    count = per_block + 2
+    count = last_count(per_block)
     i = lax.axis_index("gx")
-    low = chosen(i, [last_span(n, at, per_block) for at in range(n)])
-    tile_stencil, carry_into = stencil_stage(n, m, half, fields)
+    low = chosen(i, [last_low(n, at, per_block) for at in range(n)])
+    tile_stencil, _ = stencil_stage(n, m, half, fields)
 
     def columns(t, width):
         return pl.ds(pl.multiple_of(t * LANES, LANES), width * LANES)
 
-    def early(q):
+    for q in range(tiles - count):
         cols = columns(jnp.where(q < low, q, q + count), 1)
-        return pltpu.make_async_copy(held.at[:, :, cols], out.at[:, :, cols], sent.at[q])
-
-    for q in range(tiles - count):
-        early(q).start()
-
-    def leave(c):
-        return pltpu.make_async_copy(
-            late.at[:, :, pl.ds(c * 2 * LANES, 2 * LANES)], out.at[:, :, columns(low + 2 * c, 2)],
-            sent.at[tiles - count + c],
-        )
-
-    carry = carry_into(low)
+        pltpu.make_async_copy(held.at[:, :, cols], out.at[:, :, cols], stored.at[0]).start()
+
+    carry = tuple(carried[at] for at in range(7))
     for q in range(count):
         values, carry = tile_stencil(low + q, carry)
         for at, value in enumerate(values):
             late[at, :, q * LANES : (q + 1) * LANES] = value
-        if q % 2:
-            leave(q // 2).start()
-    for q in range(tiles - count):
-        early(q).wait()
-    for c in range(count // 2):
-        leave(c).wait()
+    pltpu.make_async_copy(late, out.at[:, :, columns(low, count)], stored.at[0]).start()
+    pltpu.make_async_copy(held, out, stored.at[0]).wait()
 
 
 def shards(n, m, conductivity):
@@ -475,43 +485,42 @@
     shape = (tiles + 1, 20, rows, LANES)
     per_block = local_cols // (2 * LANES)
     result = jax.ShapeDtypeStruct((9, half, tiles * LANES), jnp.float32)
-    fields, held = pl.pallas_call(
+    fields, held, carried = pl.pallas_call(
         functools.partial(coarse_kernel, n, m),
-        out_shape=(jax.ShapeDtypeStruct(shape, jnp.float32), result),
+        out_shape=(
+            jax.ShapeDtypeStruct(shape, jnp.float32),
+            result,
+            jax.ShapeDtypeStruct((7, rows, LANES), jnp.float32),
+        ),
         in_specs=[anywhere],
-        out_specs=(vmem, vmem),
+        out_specs=(vmem, vmem, vmem),
         scratch_shapes=[
-            pltpu.VMEM((n, planes, band, local_cols), jnp.bfloat16),
-            pltpu.VMEM((n, 8, local_cols), jnp.bfloat16),
-            pltpu.VMEM((n, planes, 8, local_cols), jnp.bfloat16),
-            pltpu.VMEM((n, planes, 8, local_cols), jnp.bfloat16),
+            pltpu.VMEM((n, 2 * band + 8, local_cols), jnp.bfloat16),
+            pltpu.VMEM((2, n - 1, planes, 8, local_cols), jnp.bfloat16),
             pltpu.VMEM((planes, 8, local_cols), jnp.bfloat16),
             pltpu.VMEM((planes, 8, local_cols), jnp.bfloat16),
             pltpu.VMEM((n, 8, local_cols), jnp.bfloat16),
-            dma((n,)),
-            dma((n,)),
-            dma((n,)),
-            dma((n,)),
+            dma((n, PIECES)),
+            dma((1,)),
             dma((2,)),
             dma((2,)),
             pltpu.SemaphoreType.REGULAR((n,)),
-            dma((2 * n + 2,)),
+            dma((2,)),
         ],
         compiler_params=pltpu.CompilerParams(
             collective_id=0, has_side_effects=True, vmem_limit_bytes=VMEM_LIMIT
         ),
         name="coarse",
     )(pltpu.with_memory_space_constraint(conductivity, pltpu.HBM))
-    count = per_block + 2
     stencil = pl.pallas_call(
         functools.partial(stencil_kernel, n, m, half, per_block),
         out_shape=result,
-        in_specs=[vmem, vmem],
+        in_specs=[vmem, vmem, vmem],
         out_specs=anywhere,
-        scratch_shapes=[pltpu.VMEM((9, half, count * LANES), jnp.float32), dma((tiles - count + count // 2,))],
+        scratch_shapes=[pltpu.VMEM((9, half, last_count(per_block) * LANES), jnp.float32), dma((1,))],
         compiler_params=pltpu.CompilerParams(vmem_limit_bytes=VMEM_LIMIT),
         name="stencil",
-    )(fields, held)
+    )(fields, held, carried)
     return stencil[:, None]
 
 

time: 18.3 us -> 18.4 us (level)
  Pallas kernels: 18.1 us -> 18.3 us
    pallas_call x1, Pallas kernels: 16.7 us -> 17.1 us  [shards(): pl.pallas_call(functools.partial(coarse_kernel, n, m), out_shape=(jax.Sha...]
    pallas_call x1, Pallas kernels: 1.4 us -> 1.19 us  [shards(): pl.pallas_call(functools.partial(stencil_kernel, n, m, half, per_block),...]
where the time goes in v3:
time: 18.4 us; the launch traced here: 18.3 us
  Pallas kernels  18.3 us (99%)
    pallas_call x1, Pallas kernels, shards(): pl.pallas_call(functools.partial(coarse_kernel, n, m), out_shape=(jax.Sha...  17.1 us
    pallas_call x1, Pallas kernels, shards(): pl.pallas_call(functools.partial(stencil_kernel, n, m, half, per_block),...  1.19 us

profile of v3, /device:TPU:0, one launch (start us, length us, event | category | flops | bytes accessed | tf_op | source)
XLA Modules:
  0.0 18.3 jit_solution(5540313952092394610)
XLA Ops:
  0.0 17.1 %coarse.1 = (f32[17,20,24,128]{3,2,1,0:T(8,128)S(1)}, f32[9,16,2048]{2,1,0:T(8,128)S(1)}, f32[7,24,128]{2,1,0:T(8,128)S(1)}) custom-call(bf16[2,128,1024]{2,1,0:T(8,128)(2,1)} %cells.1), custom_call_target="tpu_custom_call" | custom-call | tf_op jit(solution)/shard_map/coarse/pallas_call | solution.py:488
  17.1 1.2 %stencil.1 = f32[9,16,2048]{2,1,0:T(8,128)} custom-call(f32[17,20,24,128]{3,2,1,0:T(8,128)S(1)} %get-tuple-element.8.fields, f32[9,16,2048]{2,1,0:T(8,128)S(1)} %get-tuple-element.9.held, f32[7,24,128]{2,1,0:T(8,128)S(1)} %get-tuple-element.10.carried), custom_call_target="tpu_custom_call" | custom-call | tf_op jit(solution)/shard_map/stencil/pallas_call | solution.py:515

commit v4 on v3

--- a/solution.py
+++ b/solution.py
@@ -9,7 +9,7 @@
 
 MESH = pl.DeviceIdType.MESH
 LANES = 128
-PIECES = 2
+LAST = 3
 VMEM_LIMIT = 16 * 1024 * 1024
 
 
@@ -20,14 +20,15 @@
     return list(range(half, i)) + list(range(half - 1)) + list(range(i + 1, n)) + [half - 1]
 
 
+def last_block(n, i):
+    return arrivals(n, i)[-1]
+
+
 def spans(n, i, per_block):
-    tiles, piece = n * per_block, per_block // PIECES
-    order = [i] + arrivals(n, i)
-    arrived = [set(range(k * per_block, (k + 1) * per_block)) for k in order[:-1]]
-    last = order[-1] * per_block
-    arrived += [set(range(last + p * piece, last + (p + 1) * piece)) for p in range(PIECES)]
+    tiles = n * per_block
     there, found = set(), []
-    for new in arrived:
+    for k in [i] + arrivals(n, i)[:-1]:
+        new = set(range(k * per_block, (k + 1) * per_block))
         there |= new
         ready = [
             t for t in range(tiles)
@@ -37,14 +38,6 @@
     return found
 
 
-def last_count(per_block):
-    return per_block // PIECES + 2
-
-
-def last_low(n, i, per_block):
-    return min(spans(n, i, per_block)[-1][0], n * per_block - last_count(per_block))
-
-
 def chosen(i, values):
     picked = values[-1]
     for at in range(len(values) - 2, -1, -1):
@@ -54,13 +47,14 @@
 
 def coarse_kernel(
     n, m, cells, fields, held, carried, blocks, rims, south_in, north_in, pack,
-    arrived, sent, edge_sent, edge_arrived, known, own,
+    arrived, around, piece, sent, edge_sent, edge_arrived, known, own,
 ):
     i = lax.axis_index("gx")
     j = lax.axis_index("gy")
     block = cells.shape[2]
     band = cells.shape[1] // n
-    width = block // PIECES
+    half = n // 2
+    per_block = block // (2 * LANES)
     has_left, has_right = i > 0, i < n - 1
     has_south, has_north = j > 0, j < m - 1
     before, after = jnp.maximum(j - 1, 0), jnp.minimum(j + 1, m - 1)
@@ -110,26 +104,54 @@
         )
 
     def cols_of(p):
-        return pl.ds(p * width, width)
-
-    def send_rows(t, p):
+        return pl.ds(p * 2 * LANES, 2 * LANES)
+
+    def send_rows(t):
+        last = i == chosen(t, [last_block(n, at) for at in range(n)])
         for plane in range(2):
+            rows = pl.ds(plane * band, band)
+
+            @pl.when(jnp.logical_not(last))
+            def _():
+                remote(cells.at[plane, rows_of(t), :], blocks.at[i, rows, :], sent.at[0], arrived.at[i], t, j).start()
+
+        @pl.when(last)
+        def _():
+            for p in range(per_block):
+                for plane in range(2):
+                    rows = pl.ds(plane * band, band)
+                    remote(
+                        cells.at[plane, rows_of(t), cols_of(p)], blocks.at[i, rows, cols_of(p)],
+                        sent.at[0], piece.at[p], t, j,
+                    ).start()
+
+    def send_halo(t):
+        def part(start, size, sem):
             remote(
-                cells.at[plane, rows_of(t), cols_of(p)], blocks.at[i, pl.ds(plane * band, band), cols_of(p)],
-                sent.at[0], arrived.at[i, p], t, j,
+                pack.at[t, pl.ds(start, size), :], blocks.at[i, pl.ds(2 * band + start, size), :],
+                sem, around.at[i], t, j,
             ).start()
 
-    def send_halo(t, p):
-        remote(
-            pack.at[t, :, cols_of(p)], blocks.at[i, pl.ds(2 * band, 8), cols_of(p)], sent.at[0], arrived.at[i, p], t, j
-        ).start()
-
-    def send(t, rows, halo):
-        for p in range(PIECES):
-            if halo:
-                send_halo(t, p)
-            if rows:
-                send_rows(t, p)
+        slim = ((i < half) != (t < half)) & (lax.rem(t, half) != 0)
+
+        @pl.when(slim)
+        def _():
+            part(4, 2, sent.at[2])
+
+        @pl.when(jnp.logical_not(slim))
+        def _():
+            part(0, 6, sent.at[1])
+
+    passes_on = lax.rem(i, half) != half - 1
+
+    def pass_on(k):
+        @pl.when(passes_on & ((i < half) != (k < half)))
+        def _():
+            for plane in range(2):
+                remote(
+                    blocks.at[k, pl.ds(plane * band + band - 2, 2), :], blocks.at[k, pl.ds(2 * band + 2 * plane, 2), :],
+                    sent.at[3], around.at[k], jnp.minimum(i + 1, n - 1), j,
+                ).start()
 
     def to_north():
         return remote(cells.at[:, pl.ds(n * band - 8, 8), :], south_in, edge_sent.at[0], edge_arrived.at[0], i, after)
@@ -149,7 +171,7 @@
 
     @pl.when(has_left)
     def _():
-        send(0, True, False)
+        send_rows(0)
 
     for t in range(n - 2, -1, -1):
         @pl.when(i > t)
@@ -168,11 +190,14 @@
     @pl.when(has_right)
     def _():
         pl.semaphore_wait(known.at[i + 1], 1)
-        send(i + 1, True, False)
 
     @pl.when(i + 1 < n - 1)
     def _():
-        send(i + 1, False, True)
+        send_halo(i + 1)
+
+    @pl.when(has_right)
+    def _():
+        send_rows(i + 1)
 
     @pl.when(has_north)
     def _():
@@ -192,29 +217,29 @@
 
     @pl.when(i + 1 == n - 1)
     def _():
-        send(n - 1, False, True)
+        send_halo(n - 1)
 
     @pl.when(has_left)
     def _():
-        send(0, False, True)
-
-    for t in range(1, n - 1):
+        send_halo(0)
+
+    for t in range(n - 2, 0, -1):
         @pl.when(i > t)
         def _():
-            send(t, True, True)
+            send_halo(t)
+            send_rows(t)
 
     for t in range(2, n):
         @pl.when(i + 1 < t)
         def _():
             pl.semaphore_wait(known.at[t], 1)
-            send(t, True, True)
+            send_halo(t)
+            send_rows(t)
 
     blocks[i, pl.ds(2 * band, 8), :] = pack[i]
 
     first = arrival_stage(n, m, band, blocks, fields)
     tile_stencil, carry_into = stencil_stage(n, m, band // 2, fields)
-    per_block = block // (2 * LANES)
-    per_piece = per_block // PIECES
     ranges = [spans(n, at, per_block) for at in range(n)]
 
     def second(step):
@@ -222,16 +247,18 @@
 
         def one(t, carry):
             values, carry = tile_stencil(t, carry)
-            cols = pl.ds(pl.multiple_of(t * LANES, LANES), LANES)
-            for at, value in enumerate(values):
-                held[at, :, cols] = value
+            hold(t, values)
             return carry
 
         lax.fori_loop(low, end, one, carry_into(low))
 
-    def await_piece(k, p):
-        landed = blocks.at[k, :, cols_of(p)]
-        remote(landed, landed, sent.at[0], arrived.at[k, p], k, j).wait_recv()
+    def hold(t, values):
+        cols = pl.ds(pl.multiple_of(t * LANES, LANES), LANES)
+        for at, value in enumerate(values):
+            held[at, :, cols] = value
+
+    def landed(ref, sem, k):
+        remote(ref, ref, sent.at[0], sem, k, j).wait_recv()
 
     mine = blocks.at[i, pl.ds(0, 2 * band), :]
     pltpu.make_async_copy(mine, mine, own.at[1]).wait()
@@ -240,23 +267,37 @@
     orders = [arrivals(n, at) for at in range(n)]
     for step in range(n - 2):
         k = chosen(i, [order[step] for order in orders])
-        for p in range(PIECES):
-            await_piece(k, p)
+        landed(blocks.at[k, pl.ds(0, 2 * band), :], arrived.at[k], k)
+        pass_on(k)
+        landed(blocks.at[k, pl.ds(2 * band, 6), :], around.at[k], k)
         first(k, 0, per_block)
         second(step + 1)
     k = chosen(i, [order[n - 2] for order in orders])
-    for p in range(PIECES):
-        if p == PIECES - 1:
-            low = chosen(i, [last_low(n, at, per_block) for at in range(n)])
-            for at, value in enumerate(carry_into(low)):
+    low = k * per_block - 1
+    carry = carry_into(low)
+    landed(blocks.at[k, pl.ds(2 * band, 6), :], around.at[k], k)
+    for p in range(per_block):
+        if p == per_block - 1:
+            for at, value in enumerate(carry):
                 carried[at] = value
-        await_piece(k, p)
-        first(k, p * per_piece, per_piece)
-        if p < PIECES - 1:
-            second(n - 1 + p)
-
-    others = blocks.at[pl.ds(0, n - 1)]
-    remote(others, others, sent.at[0], arrived.at[0, 0], i, j).wait_send()
+        landed(blocks.at[k, pl.ds(0, 2 * band), cols_of(p)], piece.at[p], k)
+        if p == per_block - 1:
+            pass_on(k)
+        first(k, p, 1)
+        if p < per_block - 1:
+            values, carry = tile_stencil(low + p, carry)
+            hold(low + p, values)
+
+    def drained(ref, sem):
+        remote(ref, ref, sem, arrived.at[0], i, j).wait_send()
+
+    drained(blocks.at[pl.ds(0, n - 1), pl.ds(0, 2 * band), :], sent.at[0])
+    drained(blocks.at[pl.ds(0, half), pl.ds(2 * band, 6), :], sent.at[1])
+    drained(blocks.at[pl.ds(0, half - 1), pl.ds(2 * band, 2), :], sent.at[2])
+
+    @pl.when(passes_on)
+    def _():
+        drained(blocks.at[pl.ds(0, half), pl.ds(2 * band, 4), :], sent.at[3])
 
     @pl.when(has_north)
     def _():
@@ -302,7 +343,7 @@
     j = lax.axis_index("gy")
     last_rows = (i == n - 1) & (j == m - 1)
 
-    taken = 2 * band + 8
+    taken = 2 * band + 6
     want = lax.broadcasted_iota(jnp.int32, (4 * rows, taken), 0)
     have = lax.broadcasted_iota(jnp.int32, (4 * rows, taken), 1)
     group = jnp.where(want >= 3 * rows, 3, jnp.where(want >= 2 * rows, 2, jnp.where(want >= rows, 1, 0)))
@@ -326,7 +367,7 @@
     def tile_terms(k, part):
         t = k * per_block + part
         cols = pl.ds(part * 2 * LANES, 2 * LANES)
-        stored = blocks[k, :, cols]
+        stored = blocks[k, pl.ds(0, taken), cols]
         picked = jnp.dot(pick_rows, stored, preferred_element_type=jnp.float32).astype(jnp.bfloat16)
         split = jnp.dot(picked, pick_cols, preferred_element_type=jnp.float32)
         a0, c0, a1, c1 = (split[g * rows : (g + 1) * rows, :LANES] for g in range(4))
@@ -452,9 +493,9 @@
 
 def stencil_kernel(n, m, half, per_block, fields, held, carried, out, late, stored):
     tiles = fields.shape[0] - 1
-    count = last_count(per_block)
     i = lax.axis_index("gx")
-    low = chosen(i, [last_low(n, at, per_block) for at in range(n)])
+    low = (chosen(i, [last_block(n, at) for at in range(n)]) + 1) * per_block - 2
+    count = LAST
     tile_stencil, _ = stencil_stage(n, m, half, fields)
 
     def columns(t, width):
@@ -500,8 +541,10 @@
             pltpu.VMEM((planes, 8, local_cols), jnp.bfloat16),
             pltpu.VMEM((planes, 8, local_cols), jnp.bfloat16),
             pltpu.VMEM((n, 8, local_cols), jnp.bfloat16),
-            dma((n, PIECES)),
-            dma((1,)),
+            dma((n,)),
+            dma((n,)),
+            dma((per_block,)),
+            dma((4,)),
             dma((2,)),
             dma((2,)),
             pltpu.SemaphoreType.REGULAR((n,)),
@@ -517,7 +560,7 @@
         out_shape=result,
         in_specs=[vmem, vmem, vmem],
         out_specs=anywhere,
-        scratch_shapes=[pltpu.VMEM((9, half, last_count(per_block) * LANES), jnp.float32), dma((1,))],
+        scratch_shapes=[pltpu.VMEM((9, half, LAST * LANES), jnp.float32), dma((1,))],
         compiler_params=pltpu.CompilerParams(vmem_limit_bytes=VMEM_LIMIT),
         name="stencil",
     )(fields, held, carried)

time: 18.4 us -> 20.9 us (1.14)
  the two profiles are of different devices: /device:TPU:0 before, /device:TPU:14 now
where the time goes in v4:
time: 20.9 us; the launch traced here: 20.7 us
  Pallas kernels  20.7 us (99%)
    pallas_call x1, Pallas kernels, shards(): pl.pallas_call(functools.partial(coarse_kernel, n, m), out_shape=(jax.Sha...  19.6 us
    pallas_call x1, Pallas kernels, shards(): pl.pallas_call(functools.partial(stencil_kernel, n, m, half, per_block),...  1.14 us

profile of v4, /device:TPU:14, one launch (start us, length us, event | category | flops | bytes accessed | tf_op | source)
XLA Modules:
  0.0 20.7 jit_solution(3432338150748701600)
XLA Ops:
  0.0 19.6 %coarse.1 = (f32[17,20,24,128]{3,2,1,0:T(8,128)S(1)}, f32[9,16,2048]{2,1,0:T(8,128)S(1)}, f32[7,24,128]{2,1,0:T(8,128)S(1)}) custom-call(bf16[2,128,1024]{2,1,0:T(8,128)(2,1)} %cells.1), custom_call_target="tpu_custom_call" | custom-call | tf_op jit(solution)/shard_map/coarse/pallas_call | solution.py:529
  19.6 1.1 %stencil.1 = f32[9,16,2048]{2,1,0:T(8,128)} custom-call(f32[17,20,24,128]{3,2,1,0:T(8,128)S(1)} %get-tuple-element.8.fields, f32[9,16,2048]{2,1,0:T(8,128)S(1)} %get-tuple-element.9.held, f32[7,24,128]{2,1,0:T(8,128)S(1)} %get-tuple-element.10.carried), custom_call_target="tpu_custom_call" | custom-call | tf_op jit(solution)/shard_map/stencil/pallas_call | solution.py:558

commit v5 on v4

--- a/solution.py
+++ b/solution.py
@@ -16,7 +16,7 @@
 def arrivals(n, i):
     half = n // 2
     if i < half:
-        return list(range(i)) + list(range(n - 1, half, -1)) + list(range(i + 1, half)) + [half]
+        return list(range(i)) + list(range(n - 1, i, -1))
     return list(range(half, i)) + list(range(half - 1)) + list(range(i + 1, n)) + [half - 1]
 
 
@@ -53,7 +53,6 @@
     j = lax.axis_index("gy")
     block = cells.shape[2]
     band = cells.shape[1] // n
-    half = n // 2
     per_block = block // (2 * LANES)
     has_left, has_right = i > 0, i < n - 1
     has_south, has_north = j > 0, j < m - 1
@@ -126,32 +125,8 @@
                     ).start()
 
     def send_halo(t):
-        def part(start, size, sem):
-            remote(
-                pack.at[t, pl.ds(start, size), :], blocks.at[i, pl.ds(2 * band + start, size), :],
-                sem, around.at[i], t, j,
-            ).start()
-
-        slim = ((i < half) != (t < half)) & (lax.rem(t, half) != 0)
-
-        @pl.when(slim)
-        def _():
-            part(4, 2, sent.at[2])
-
-        @pl.when(jnp.logical_not(slim))
-        def _():
-            part(0, 6, sent.at[1])
-
-    passes_on = lax.rem(i, half) != half - 1
-
-    def pass_on(k):
-        @pl.when(passes_on & ((i < half) != (k < half)))
-        def _():
-            for plane in range(2):
-                remote(
-                    blocks.at[k, pl.ds(plane * band + band - 2, 2), :], blocks.at[k, pl.ds(2 * band + 2 * plane, 2), :],
-                    sent.at[3], around.at[k], jnp.minimum(i + 1, n - 1), j,
-                ).start()
+        rows = pl.ds(2 * band, 6)
+        remote(pack.at[t, pl.ds(0, 6), :], blocks.at[i, rows, :], sent.at[1], around.at[i], t, j).start()
 
     def to_north():
         return remote(cells.at[:, pl.ds(n * band - 8, 8), :], south_in, edge_sent.at[0], edge_arrived.at[0], i, after)
@@ -238,7 +213,7 @@
 
     blocks[i, pl.ds(2 * band, 8), :] = pack[i]
 
-    first = arrival_stage(n, m, band, blocks, fields)
+    tile_terms, first = arrival_stage(n, m, band, blocks, fields)
     tile_stencil, carry_into = stencil_stage(n, m, band // 2, fields)
     ranges = [spans(n, at, per_block) for at in range(n)]
 
@@ -268,7 +243,6 @@
     for step in range(n - 2):
         k = chosen(i, [order[step] for order in orders])
         landed(blocks.at[k, pl.ds(0, 2 * band), :], arrived.at[k], k)
-        pass_on(k)
         landed(blocks.at[k, pl.ds(2 * band, 6), :], around.at[k], k)
         first(k, 0, per_block)
         second(step + 1)
@@ -277,27 +251,22 @@
     carry = carry_into(low)
     landed(blocks.at[k, pl.ds(2 * band, 6), :], around.at[k], k)
     for p in range(per_block):
+        landed(blocks.at[k, pl.ds(0, 2 * band), cols_of(p)], piece.at[p], k)
+        if p:
+            values, carry = tile_stencil(low + p - 1, carry)
+        store = tile_terms(k, p)
+        if p:
+            hold(low + p - 1, values)
         if p == per_block - 1:
             for at, value in enumerate(carry):
                 carried[at] = value
-        landed(blocks.at[k, pl.ds(0, 2 * band), cols_of(p)], piece.at[p], k)
-        if p == per_block - 1:
-            pass_on(k)
-        first(k, p, 1)
-        if p < per_block - 1:
-            values, carry = tile_stencil(low + p, carry)
-            hold(low + p, values)
+        store()
 
     def drained(ref, sem):
         remote(ref, ref, sem, arrived.at[0], i, j).wait_send()
 
     drained(blocks.at[pl.ds(0, n - 1), pl.ds(0, 2 * band), :], sent.at[0])
-    drained(blocks.at[pl.ds(0, half), pl.ds(2 * band, 6), :], sent.at[1])
-    drained(blocks.at[pl.ds(0, half - 1), pl.ds(2 * band, 2), :], sent.at[2])
-
-    @pl.when(passes_on)
-    def _():
-        drained(blocks.at[pl.ds(0, half), pl.ds(2 * band, 4), :], sent.at[3])
+    drained(blocks.at[pl.ds(0, n - 1), pl.ds(2 * band, 6), :], sent.at[1])
 
     @pl.when(has_north)
     def _():
@@ -382,20 +351,23 @@
         side_a, side_b, side_c, side_d = (
             (x + ((k0 + k1) + v)) - v for x, (k0, k1), v in zip((h1, h1, g1, g1), pairs, verticals(pairs))
         )
-        for at, value in enumerate(
-            (a0, a1, c0, c1, s0, n0, b0, b1, d0, d1, t0, s1, n1, t1, h1, g1, side_a, side_b, side_c, side_d)
-        ):
-            fields[t, at] = value
+        values = (a0, a1, c0, c1, s0, n0, b0, b1, d0, d1, t0, s1, n1, t1, h1, g1, side_a, side_b, side_c, side_d)
+
+        def store():
+            for at, value in enumerate(values):
+                fields[t, at] = value
+
+        return store
 
     def first(k, start, count):
         for part in range(start, start + count):
-            tile_terms(k, part)
+            tile_terms(k, part)()
 
     ones = jnp.ones((rows, LANES), jnp.float32)
     for at in range(6):
         fields[tiles, at] = ones
 
-    return first
+    return tile_terms, first
 
 
 def stencil_stage(n, m, half, fields):
@@ -544,7 +516,7 @@
             dma((n,)),
             dma((n,)),
             dma((per_block,)),
-            dma((4,)),
+            dma((2,)),
             dma((2,)),
             dma((2,)),
             pltpu.SemaphoreType.REGULAR((n,)),

time: 20.9 us -> 18.6 us (0.89)
  the two profiles are of different devices: /device:TPU:14 before, /device:TPU:10 now
where the time goes in v5:
time: 18.6 us; the launch traced here: 18.4 us
  Pallas kernels  18.4 us (99%)
    pallas_call x1, Pallas kernels, shards(): pl.pallas_call(functools.partial(coarse_kernel, n, m), out_shape=(jax.Sha...  17.3 us
    pallas_call x1, Pallas kernels, shards(): pl.pallas_call(functools.partial(stencil_kernel, n, m, half, per_block),...  1.14 us

profile of v5, /device:TPU:10, one launch (start us, length us, event | category | flops | bytes accessed | tf_op | source)
XLA Modules:
  0.0 18.4 jit_solution(15871189342130387838)
XLA Ops:
  0.0 17.3 %coarse.1 = (f32[17,20,24,128]{3,2,1,0:T(8,128)S(1)}, f32[9,16,2048]{2,1,0:T(8,128)S(1)}, f32[7,24,128]{2,1,0:T(8,128)S(1)}) custom-call(bf16[2,128,1024]{2,1,0:T(8,128)(2,1)} %cells.1), custom_call_target="tpu_custom_call" | custom-call | tf_op jit(solution)/shard_map/coarse/pallas_call | solution.py:501
  17.3 1.1 %stencil.1 = f32[9,16,2048]{2,1,0:T(8,128)} custom-call(f32[17,20,24,128]{3,2,1,0:T(8,128)S(1)} %get-tuple-element.8.fields, f32[9,16,2048]{2,1,0:T(8,128)S(1)} %get-tuple-element.9.held, f32[7,24,128]{2,1,0:T(8,128)S(1)} %get-tuple-element.10.carried), custom_call_target="tpu_custom_call" | custom-call | tf_op jit(solution)/shard_map/stencil/pallas_call | solution.py:530

commit v6 on v5

--- a/solution.py
+++ b/solution.py
@@ -53,6 +53,7 @@
     j = lax.axis_index("gy")
     block = cells.shape[2]
     band = cells.shape[1] // n
+    half = n // 2
     per_block = block // (2 * LANES)
     has_left, has_right = i > 0, i < n - 1
     has_south, has_north = j > 0, j < m - 1
@@ -71,11 +72,9 @@
     def _():
         signal(barrier, i, after)
 
-    first_of_all = (i == 0) & (j == 0)
-
-    @pl.when((i == 0) & (j == 1))
-    def _():
-        signal(barrier, 0, 0)
+    @pl.when(has_left & (i <= half))
+    def _():
+        signal(barrier, i - 1, j)
 
     def rows_of(t):
         return pl.ds(pl.multiple_of(t * band, band), band)
@@ -105,9 +104,9 @@
     def cols_of(p):
         return pl.ds(p * 2 * LANES, 2 * LANES)
 
-    def send_rows(t):
+    def send_rows(t, planes=(0, 1)):
         last = i == chosen(t, [last_block(n, at) for at in range(n)])
-        for plane in range(2):
+        for plane in planes:
             rows = pl.ds(plane * band, band)
 
             @pl.when(jnp.logical_not(last))
@@ -117,7 +116,7 @@
         @pl.when(last)
         def _():
             for p in range(per_block):
-                for plane in range(2):
+                for plane in planes:
                     rows = pl.ds(plane * band, band)
                     remote(
                         cells.at[plane, rows_of(t), cols_of(p)], blocks.at[i, rows, cols_of(p)],
@@ -142,14 +141,18 @@
         rows = jnp.where(sub < 2, low[0], jnp.where(sub < 4, low[1], jnp.where(sub == 4, high[0], high[1])))
         pack[t] = rows.astype(jnp.bfloat16)
 
-    pl.semaphore_wait(barrier, i + jnp.where(has_south | first_of_all, 1, 0))
+    pl.semaphore_wait(barrier, i + jnp.where(has_south, 1, 0) + jnp.where(i < half, 1, 0))
 
     @pl.when(has_left)
     def _():
         send_rows(0)
 
+    @pl.when(i < half)
+    def _():
+        send_rows(i + 1)
+
     for t in range(n - 2, -1, -1):
-        @pl.when(i > t)
+        @pl.when((i > t) & ((i > t + 1) | (i > half)))
         def _():
             signal(known.at[i], t, j)
 
@@ -162,16 +165,13 @@
     for t in range(1, n - 1):
         make_pack(t, rims.at[0, t - 1], rims.at[1, t])
 
-    @pl.when(has_right)
+    @pl.when(i + 1 < n - 1)
+    def _():
+        send_halo(i + 1)
+
+    @pl.when(has_right & (i >= half))
     def _():
         pl.semaphore_wait(known.at[i + 1], 1)
-
-    @pl.when(i + 1 < n - 1)
-    def _():
-        send_halo(i + 1)
-
-    @pl.when(has_right)
-    def _():
         send_rows(i + 1)
 
     @pl.when(has_north)
@@ -198,11 +198,22 @@
     def _():
         send_halo(0)
 
-    for t in range(n - 2, 0, -1):
-        @pl.when(i > t)
+    splits = i > half
+
+    @pl.when(splits)
+    def _():
+        send_rows(i - 1, (0,))
+
+    for t in range(1, n - 1):
+        @pl.when((i > t) & jnp.logical_not(splits & (i == t + 1)))
         def _():
             send_halo(t)
             send_rows(t)
+
+    @pl.when(splits)
+    def _():
+        send_halo(i - 1)
+        send_rows(i - 1, (1,))
 
     for t in range(2, n):
         @pl.when(i + 1 < t)
@@ -218,14 +229,13 @@
     ranges = [spans(n, at, per_block) for at in range(n)]
 
     def second(step):
-        low, end = (chosen(i, [found[step][side] for found in ranges]) for side in range(2))
-
-        def one(t, carry):
-            values, carry = tile_stencil(t, carry)
-            hold(t, values)
-            return carry
-
-        lax.fori_loop(low, end, one, carry_into(low))
+        found = [of_device[step] for of_device in ranges]
+        count = max(end - low for low, end in found)
+        low = chosen(i, [min(low, n * per_block - count) for low, _ in found])
+        carry = carry_into(low)
+        for q in range(count):
+            values, carry = tile_stencil(low + q, carry)
+            hold(low + q, values)
 
     def hold(t, values):
         cols = pl.ds(pl.multiple_of(t * LANES, LANES), LANES)
@@ -250,17 +260,23 @@
     low = k * per_block - 1
     carry = carry_into(low)
     landed(blocks.at[k, pl.ds(2 * band, 6), :], around.at[k], k)
-    for p in range(per_block):
-        landed(blocks.at[k, pl.ds(0, 2 * band), cols_of(p)], piece.at[p], k)
-        if p:
-            values, carry = tile_stencil(low + p - 1, carry)
-        store = tile_terms(k, p)
-        if p:
-            hold(low + p - 1, values)
-        if p == per_block - 1:
+    done = 0
+    for group in [range(per_block - 2)] + [(p,) for p in range(per_block - 2, per_block)]:
+        for p in group:
+            landed(blocks.at[k, pl.ds(0, 2 * band), cols_of(p)], piece.at[p], k)
+        between = []
+        for q in range(done, group[0]):
+            values, carry = tile_stencil(low + q, carry)
+            between.append((low + q, values))
+        done = group[0]
+        stores = [tile_terms(k, p) for p in group]
+        for t, values in between:
+            hold(t, values)
+        if group[-1] == per_block - 1:
             for at, value in enumerate(carry):
                 carried[at] = value
-        store()
+        for store in stores:
+            store()
 
     def drained(ref, sem):
         remote(ref, ref, sem, arrived.at[0], i, j).wait_send()

time: 18.6 us -> 19.1 us (1.027)
  the two profiles are of different devices: /device:TPU:10 before, /device:TPU:0 now
where the time goes in v6:
time: 19.1 us; the launch traced here: 19 us
  Pallas kernels  19 us (99%)
    pallas_call x1, Pallas kernels, shards(): pl.pallas_call(functools.partial(coarse_kernel, n, m), out_shape=(jax.Sha...  17.8 us
    pallas_call x1, Pallas kernels, shards(): pl.pallas_call(functools.partial(stencil_kernel, n, m, half, per_block),...  1.14 us

profile of v6, /device:TPU:0, one launch (start us, length us, event | category | flops | bytes accessed | tf_op | source)
XLA Modules:
  0.0 19.0 jit_solution(14574562453136314844)
XLA Ops:
  0.0 17.8 %coarse.1 = (f32[17,20,24,128]{3,2,1,0:T(8,128)S(1)}, f32[9,16,2048]{2,1,0:T(8,128)S(1)}, f32[7,24,128]{2,1,0:T(8,128)S(1)}) custom-call(bf16[2,128,1024]{2,1,0:T(8,128)(2,1)} %cells.1), custom_call_target="tpu_custom_call" | custom-call | tf_op jit(solution)/shard_map/coarse/pallas_call | solution.py:517
  17.8 1.1 %stencil.1 = f32[9,16,2048]{2,1,0:T(8,128)} custom-call(f32[17,20,24,128]{3,2,1,0:T(8,128)S(1)} %get-tuple-element.8.fields, f32[9,16,2048]{2,1,0:T(8,128)S(1)} %get-tuple-element.9.held, f32[7,24,128]{2,1,0:T(8,128)S(1)} %get-tuple-element.10.carried), custom_call_target="tpu_custom_call" | custom-call | tf_op jit(solution)/shard_map/stencil/pallas_call | solution.py:546

commit v7 on v6

--- a/solution.py
+++ b/solution.py
@@ -16,7 +16,7 @@
 def arrivals(n, i):
     half = n // 2
     if i < half:
-        return list(range(i)) + list(range(n - 1, i, -1))
+        return list(range(i)) + list(range(n - 1, half, -1)) + list(range(i + 1, half)) + [half]
     return list(range(half, i)) + list(range(half - 1)) + list(range(i + 1, n)) + [half - 1]
 
 
@@ -63,6 +63,11 @@
         pl.semaphore_signal(sem, inc=1, device_id=(x, y), device_id_type=MESH)
 
     barrier = pltpu.get_barrier_semaphore()
+
+    @pl.when(has_left & (i <= half))
+    def _():
+        signal(barrier, i - 1, j)
+
     for t in range(1, n):
         @pl.when(i < t)
         def _():
@@ -71,10 +76,6 @@
     @pl.when(has_north)
     def _():
         signal(barrier, i, after)
-
-    @pl.when(has_left & (i <= half))
-    def _():
-        signal(barrier, i - 1, j)
 
     def rows_of(t):
         return pl.ds(pl.multiple_of(t * band, band), band)
@@ -104,9 +105,9 @@
     def cols_of(p):
         return pl.ds(p * 2 * LANES, 2 * LANES)
 
-    def send_rows(t, planes=(0, 1)):
+    def send_rows(t, planes=(0, 1), pieces=range(per_block)):
         last = i == chosen(t, [last_block(n, at) for at in range(n)])
-        for plane in planes:
+        for plane in planes if pieces[0] == 0 else ():
             rows = pl.ds(plane * band, band)
 
             @pl.when(jnp.logical_not(last))
@@ -115,7 +116,7 @@
 
         @pl.when(last)
         def _():
-            for p in range(per_block):
+            for p in pieces:
                 for plane in planes:
                     rows = pl.ds(plane * band, band)
                     remote(
@@ -145,7 +146,7 @@
 
     @pl.when(has_left)
     def _():
-        send_rows(0)
+        send_rows(0, pieces=range(per_block // 2))
 
     @pl.when(i < half)
     def _():
@@ -197,6 +198,7 @@
     @pl.when(has_left)
     def _():
         send_halo(0)
+        send_rows(0, pieces=range(per_block // 2, per_block))
 
     splits = i > half
 

time: 19.1 us -> 17.6 us (0.921)
  Pallas kernels: 19 us -> 17.3 us
    pallas_call x1, Pallas kernels: 17.8 us -> 16.2 us  [shards(): pl.pallas_call(functools.partial(coarse_kernel, n, m), out_shape=(jax.Sha...]
where the time goes in v7:
time: 17.6 us; the launch traced here: 17.4 us
  Pallas kernels  17.3 us (98%)
    pallas_call x1, Pallas kernels, shards(): pl.pallas_call(functools.partial(coarse_kernel, n, m), out_shape=(jax.Sha...  16.2 us
    pallas_call x1, Pallas kernels, shards(): pl.pallas_call(functools.partial(stencil_kernel, n, m, half, per_block),...  1.14 us

profile of v7, /device:TPU:0, one launch (start us, length us, event | category | flops | bytes accessed | tf_op | source)
XLA Modules:
  0.0 17.4 jit_solution(12049036362964835678)
XLA Ops:
  0.0 16.2 %coarse.1 = (f32[17,20,24,128]{3,2,1,0:T(8,128)S(1)}, f32[9,16,2048]{2,1,0:T(8,128)S(1)}, f32[7,24,128]{2,1,0:T(8,128)S(1)}) custom-call(bf16[2,128,1024]{2,1,0:T(8,128)(2,1)} %cells.1), custom_call_target="tpu_custom_call" | custom-call | tf_op jit(solution)/shard_map/coarse/pallas_call | solution.py:519
  16.2 1.1 %stencil.1 = f32[9,16,2048]{2,1,0:T(8,128)} custom-call(f32[17,20,24,128]{3,2,1,0:T(8,128)S(1)} %get-tuple-element.8.fields, f32[9,16,2048]{2,1,0:T(8,128)S(1)} %get-tuple-element.9.held, f32[7,24,128]{2,1,0:T(8,128)S(1)} %get-tuple-element.10.carried), custom_call_target="tpu_custom_call" | custom-call | tf_op jit(solution)/shard_map/stencil/pallas_call | solution.py:548

commit v8 on v7

--- a/solution.py
+++ b/solution.py
@@ -64,9 +64,9 @@
 
     barrier = pltpu.get_barrier_semaphore()
 
-    @pl.when(has_left & (i <= half))
-    def _():
-        signal(barrier, i - 1, j)
+    @pl.when(i == 1)
+    def _():
+        signal(barrier, 0, j)
 
     for t in range(1, n):
         @pl.when(i < t)
@@ -142,18 +142,18 @@
         rows = jnp.where(sub < 2, low[0], jnp.where(sub < 4, low[1], jnp.where(sub == 4, high[0], high[1])))
         pack[t] = rows.astype(jnp.bfloat16)
 
-    pl.semaphore_wait(barrier, i + jnp.where(has_south, 1, 0) + jnp.where(i < half, 1, 0))
+    pl.semaphore_wait(barrier, i + jnp.where(has_south, 1, 0) + jnp.where(i == 0, 1, 0))
 
     @pl.when(has_left)
     def _():
-        send_rows(0, pieces=range(per_block // 2))
-
-    @pl.when(i < half)
-    def _():
-        send_rows(i + 1)
+        send_rows(0, pieces=range(per_block - 1))
+
+    @pl.when(i == 0)
+    def _():
+        send_rows(1)
 
     for t in range(n - 2, -1, -1):
-        @pl.when((i > t) & ((i > t + 1) | (i > half)))
+        @pl.when((i > t) & ((t > 0) | (i > 1)))
         def _():
             signal(known.at[i], t, j)
 
@@ -166,20 +166,39 @@
     for t in range(1, n - 1):
         make_pack(t, rims.at[0, t - 1], rims.at[1, t])
 
+    @pl.when(has_right & (i > 0))
+    def _():
+        pl.semaphore_wait(known.at[i + 1], 1)
+
     @pl.when(i + 1 < n - 1)
     def _():
         send_halo(i + 1)
 
-    @pl.when(has_right & (i >= half))
-    def _():
-        pl.semaphore_wait(known.at[i + 1], 1)
+    @pl.when(has_right & (i > 0))
+    def _():
         send_rows(i + 1)
+
+    splits = i > half
+
+    @pl.when(splits)
+    def _():
+        send_rows(i - 1, (0,))
 
     @pl.when(has_north)
     def _():
         pl.semaphore_wait(known.at[0], 1)
         to_north().start()
 
+    for t in range(2, n):
+        @pl.when(i + 1 < t)
+        def _():
+            pl.semaphore_wait(known.at[t], 1)
+            if t < n - 1:
+                send_halo(t)
+                send_rows(t)
+            else:
+                send_rows(t, pieces=range(per_block // 2))
+
     @pl.when(has_south)
     def _():
         to_north().wait_recv()
@@ -191,20 +210,18 @@
     make_pack(0, south_in, rims.at[1, 0])
     make_pack(n - 1, rims.at[0, n - 2], north_in)
 
-    @pl.when(i + 1 == n - 1)
+    @pl.when(has_left)
+    def _():
+        send_halo(0)
+        send_rows(0, pieces=range(per_block - 1, per_block))
+
+    @pl.when(has_right)
     def _():
         send_halo(n - 1)
 
-    @pl.when(has_left)
-    def _():
-        send_halo(0)
-        send_rows(0, pieces=range(per_block // 2, per_block))
-
-    splits = i > half
-
-    @pl.when(splits)
-    def _():
-        send_rows(i - 1, (0,))
+    @pl.when(i + 1 < n - 1)
+    def _():
+        send_rows(n - 1, pieces=range(per_block // 2, per_block))
 
     for t in range(1, n - 1):
         @pl.when((i > t) & jnp.logical_not(splits & (i == t + 1)))
@@ -216,13 +233,6 @@
     def _():
         send_halo(i - 1)
         send_rows(i - 1, (1,))
-
-    for t in range(2, n):
-        @pl.when(i + 1 < t)
-        def _():
-            pl.semaphore_wait(known.at[t], 1)
-            send_halo(t)
-            send_rows(t)
 
     blocks[i, pl.ds(2 * band, 8), :] = pack[i]
 
@@ -489,11 +499,17 @@
     tile_stencil, _ = stencil_stage(n, m, half, fields)
 
     def columns(t, width):
-        return pl.ds(pl.multiple_of(t * LANES, LANES), width * LANES)
-
-    for q in range(tiles - count):
-        cols = columns(jnp.where(q < low, q, q + count), 1)
-        pltpu.make_async_copy(held.at[:, :, cols], out.at[:, :, cols], stored.at[0]).start()
+        start = t * LANES
+        return pl.ds(start if isinstance(t, int) else pl.multiple_of(start, LANES), width * LANES)
+
+    for block in sorted({last_block(n, at) for at in range(n)}):
+        at = (block + 1) * per_block - 2
+
+        @pl.when(low == at)
+        def _():
+            for start in [*range(0, at, 5), *range(at + count, tiles, 5)]:
+                cols = columns(start, min(5, (at if start < at else tiles) - start))
+                pltpu.make_async_copy(held.at[:, :, cols], out.at[:, :, cols], stored.at[0]).start()
 
     carry = tuple(carried[at] for at in range(7))
     for q in range(count):

time: 17.6 us -> 17.4 us (0.989)
  no operation moved by 1% of the time
where the time goes in v8:
time: 17.4 us; the launch traced here: 17.3 us
  Pallas kernels  17.3 us (99%)
    pallas_call x1, Pallas kernels, shards(): pl.pallas_call(functools.partial(coarse_kernel, n, m), out_shape=(jax.Sha...  16 us
    pallas_call x1, Pallas kernels, shards(): pl.pallas_call(functools.partial(stencil_kernel, n, m, half, per_block),...  1.21 us

profile of v8, /device:TPU:0, one launch (start us, length us, event | category | flops | bytes accessed | tf_op | source)
XLA Modules:
  0.0 17.3 jit_solution(16405860507821405154)
XLA Ops:
  0.0 16.0 %coarse.1 = (f32[17,20,24,128]{3,2,1,0:T(8,128)S(1)}, f32[9,16,2048]{2,1,0:T(8,128)S(1)}, f32[7,24,128]{2,1,0:T(8,128)S(1)}) custom-call(bf16[2,128,1024]{2,1,0:T(8,128)(2,1)} %cells.1), custom_call_target="tpu_custom_call" | custom-call | tf_op jit(solution)/shard_map/coarse/pallas_call | solution.py:535
  16.1 1.2 %stencil.1 = f32[9,16,2048]{2,1,0:T(8,128)} custom-call(f32[17,20,24,128]{3,2,1,0:T(8,128)S(1)} %get-tuple-element.8.fields, f32[9,16,2048]{2,1,0:T(8,128)S(1)} %get-tuple-element.9.held, f32[7,24,128]{2,1,0:T(8,128)S(1)} %get-tuple-element.10.carried), custom_call_target="tpu_custom_call" | custom-call | tf_op jit(solution)/shard_map/stencil/pallas_call | solution.py:564

commit v9 on v8

--- a/solution.py
+++ b/solution.py
@@ -102,12 +102,14 @@
             src_ref=src, dst_ref=dst, send_sem=send, recv_sem=recv, device_id=(x, y), device_id_type=MESH
         )
 
-    def cols_of(p):
-        return pl.ds(p * 2 * LANES, 2 * LANES)
-
-    def send_rows(t, planes=(0, 1), pieces=range(per_block)):
+    groups = tuple(enumerate([range(per_block - 2), *((p,) for p in range(per_block - 2, per_block))]))
+
+    def cols_of(group):
+        return pl.ds(group[0] * 2 * LANES, len(group) * 2 * LANES)
+
+    def send_rows(t, planes=(0, 1), pieces=groups):
         last = i == chosen(t, [last_block(n, at) for at in range(n)])
-        for plane in planes if pieces[0] == 0 else ():
+        for plane in planes if pieces[0] == groups[0] else ():
             rows = pl.ds(plane * band, band)
 
             @pl.when(jnp.logical_not(last))
@@ -116,11 +118,11 @@
 
         @pl.when(last)
         def _():
-            for p in pieces:
+            for p, group in pieces:
                 for plane in planes:
                     rows = pl.ds(plane * band, band)
                     remote(
-                        cells.at[plane, rows_of(t), cols_of(p)], blocks.at[i, rows, cols_of(p)],
+                        cells.at[plane, rows_of(t), cols_of(group)], blocks.at[i, rows, cols_of(group)],
                         sent.at[0], piece.at[p], t, j,
                     ).start()
 
@@ -144,18 +146,18 @@
 
     pl.semaphore_wait(barrier, i + jnp.where(has_south, 1, 0) + jnp.where(i == 0, 1, 0))
 
-    @pl.when(has_left)
-    def _():
-        send_rows(0, pieces=range(per_block - 1))
-
-    @pl.when(i == 0)
-    def _():
-        send_rows(1)
-
     for t in range(n - 2, -1, -1):
         @pl.when((i > t) & ((t > 0) | (i > 1)))
         def _():
-            signal(known.at[i], t, j)
+            signal(known.at[i - 1], t, j)
+
+    @pl.when(has_left)
+    def _():
+        send_rows(0, pieces=groups[:2])
+
+    @pl.when(i == 0)
+    def _():
+        send_rows(1)
 
     @pl.when(has_south)
     def _():
@@ -168,7 +170,7 @@
 
     @pl.when(has_right & (i > 0))
     def _():
-        pl.semaphore_wait(known.at[i + 1], 1)
+        pl.semaphore_wait(known.at[i], 1)
 
     @pl.when(i + 1 < n - 1)
     def _():
@@ -192,12 +194,12 @@
     for t in range(2, n):
         @pl.when(i + 1 < t)
         def _():
-            pl.semaphore_wait(known.at[t], 1)
+            pl.semaphore_wait(known.at[t - 1], 1)
             if t < n - 1:
                 send_halo(t)
                 send_rows(t)
             else:
-                send_rows(t, pieces=range(per_block // 2))
+                send_rows(t, pieces=groups[:1])
 
     @pl.when(has_south)
     def _():
@@ -213,7 +215,7 @@
     @pl.when(has_left)
     def _():
         send_halo(0)
-        send_rows(0, pieces=range(per_block - 1, per_block))
+        send_rows(0, pieces=groups[2:])
 
     @pl.when(has_right)
     def _():
@@ -221,7 +223,7 @@
 
     @pl.when(i + 1 < n - 1)
     def _():
-        send_rows(n - 1, pieces=range(per_block // 2, per_block))
+        send_rows(n - 1, pieces=groups[1:])
 
     for t in range(1, n - 1):
         @pl.when((i > t) & jnp.logical_not(splits & (i == t + 1)))
@@ -273,9 +275,8 @@
     carry = carry_into(low)
     landed(blocks.at[k, pl.ds(2 * band, 6), :], around.at[k], k)
     done = 0
-    for group in [range(per_block - 2)] + [(p,) for p in range(per_block - 2, per_block)]:
-        for p in group:
-            landed(blocks.at[k, pl.ds(0, 2 * band), cols_of(p)], piece.at[p], k)
+    for p, group in groups:
+        landed(blocks.at[k, pl.ds(0, 2 * band), cols_of(group)], piece.at[p], k)
         between = []
         for q in range(done, group[0]):
             values, carry = tile_stencil(low + q, carry)
@@ -294,6 +295,7 @@
         remote(ref, ref, sem, arrived.at[0], i, j).wait_send()
 
     drained(blocks.at[pl.ds(0, n - 1), pl.ds(0, 2 * band), :], sent.at[0])
+
     drained(blocks.at[pl.ds(0, n - 1), pl.ds(2 * band, 6), :], sent.at[1])
 
     @pl.when(has_north)
@@ -499,17 +501,11 @@
     tile_stencil, _ = stencil_stage(n, m, half, fields)
 
     def columns(t, width):
-        start = t * LANES
-        return pl.ds(start if isinstance(t, int) else pl.multiple_of(start, LANES), width * LANES)
-
-    for block in sorted({last_block(n, at) for at in range(n)}):
-        at = (block + 1) * per_block - 2
-
-        @pl.when(low == at)
-        def _():
-            for start in [*range(0, at, 5), *range(at + count, tiles, 5)]:
-                cols = columns(start, min(5, (at if start < at else tiles) - start))
-                pltpu.make_async_copy(held.at[:, :, cols], out.at[:, :, cols], stored.at[0]).start()
+        return pl.ds(pl.multiple_of(t * LANES, LANES), width * LANES)
+
+    for q in range(0, tiles - count, 2):
+        cols = columns(jnp.where(q < low, q, q + count), min(2, tiles - count - q))
+        pltpu.make_async_copy(held.at[:, :, cols], out.at[:, :, cols], stored.at[0]).start()
 
     carry = tuple(carried[at] for at in range(7))
     for q in range(count):
@@ -549,11 +545,11 @@
             pltpu.VMEM((n, 8, local_cols), jnp.bfloat16),
             dma((n,)),
             dma((n,)),
-            dma((per_block,)),
+            dma((3,)),
             dma((2,)),
             dma((2,)),
             dma((2,)),
-            pltpu.SemaphoreType.REGULAR((n,)),
+            pltpu.SemaphoreType.REGULAR((n - 1,)),
             dma((2,)),
         ],
         compiler_params=pltpu.CompilerParams(

time: 17.4 us -> 17.3 us (level)
  Pallas kernels: 17.3 us -> 17.1 us
where the time goes in v9:
time: 17.3 us; the launch traced here: 17.1 us
  Pallas kernels  17.1 us (99%)
    pallas_call x1, Pallas kernels, shards(): pl.pallas_call(functools.partial(coarse_kernel, n, m), out_shape=(jax.Sha...  16 us
    pallas_call x1, Pallas kernels, shards(): pl.pallas_call(functools.partial(stencil_kernel, n, m, half, per_block),...  1.09 us

profile of v9, /device:TPU:0, one launch (start us, length us, event | category | flops | bytes accessed | tf_op | source)
XLA Modules:
  0.0 17.1 jit_solution(2884989044686185285)
XLA Ops:
  0.0 16.0 %coarse.1 = (f32[17,20,24,128]{3,2,1,0:T(8,128)S(1)}, f32[9,16,2048]{2,1,0:T(8,128)S(1)}, f32[7,24,128]{2,1,0:T(8,128)S(1)}) custom-call(bf16[2,128,1024]{2,1,0:T(8,128)(2,1)} %cells.1), custom_call_target="tpu_custom_call" | custom-call | tf_op jit(solution)/shard_map/coarse/pallas_call | solution.py:531
  16.0 1.1 %stencil.1 = f32[9,16,2048]{2,1,0:T(8,128)} custom-call(f32[17,20,24,128]{3,2,1,0:T(8,128)S(1)} %get-tuple-element.8.fields, f32[9,16,2048]{2,1,0:T(8,128)S(1)} %get-tuple-element.9.held, f32[7,24,128]{2,1,0:T(8,128)S(1)} %get-tuple-element.10.carried), custom_call_target="tpu_custom_call" | custom-call | tf_op jit(solution)/shard_map/stencil/pallas_call | solution.py:560

commit v10 on v9

--- a/solution.py
+++ b/solution.py
@@ -109,22 +109,20 @@
 
     def send_rows(t, planes=(0, 1), pieces=groups):
         last = i == chosen(t, [last_block(n, at) for at in range(n)])
-        for plane in planes if pieces[0] == groups[0] else ():
-            rows = pl.ds(plane * band, band)
-
+        low, count = planes[0], len(planes)
+        rows = blocks.at[i, pl.ds(low * band, count * band), :].reshape(count, band, block)
+        taken = cells.at[pl.ds(low, count), rows_of(t), :]
+
+        if pieces[0] == groups[0]:
             @pl.when(jnp.logical_not(last))
             def _():
-                remote(cells.at[plane, rows_of(t), :], blocks.at[i, rows, :], sent.at[0], arrived.at[i], t, j).start()
+                remote(taken, rows, sent.at[0], arrived.at[i], t, j).start()
 
         @pl.when(last)
         def _():
             for p, group in pieces:
-                for plane in planes:
-                    rows = pl.ds(plane * band, band)
-                    remote(
-                        cells.at[plane, rows_of(t), cols_of(group)], blocks.at[i, rows, cols_of(group)],
-                        sent.at[0], piece.at[p], t, j,
-                    ).start()
+                cols = cols_of(group)
+                remote(taken.at[:, :, cols], rows.at[:, :, cols], sent.at[0], piece.at[p], t, j).start()
 
     def send_halo(t):
         rows = pl.ds(2 * band, 6)

time: 17.3 us -> 17.3 us (level)
  no operation moved by 1% of the time
where the time goes in v10:
time: 17.3 us; the launch traced here: 17.1 us
  Pallas kernels  17.1 us (99%)
    pallas_call x1, Pallas kernels, shards(): pl.pallas_call(functools.partial(coarse_kernel, n, m), out_shape=(jax.Sha...  16 us
    pallas_call x1, Pallas kernels, shards(): pl.pallas_call(functools.partial(stencil_kernel, n, m, half, per_block),...  1.09 us

profile of v10, /device:TPU:0, one launch (start us, length us, event | category | flops | bytes accessed | tf_op | source)
XLA Modules:
  0.0 17.1 jit_solution(5467771144950342312)
XLA Ops:
  0.0 16.0 %coarse.1 = (f32[17,20,24,128]{3,2,1,0:T(8,128)S(1)}, f32[9,16,2048]{2,1,0:T(8,128)S(1)}, f32[7,24,128]{2,1,0:T(8,128)S(1)}) custom-call(bf16[2,128,1024]{2,1,0:T(8,128)(2,1)} %cells.1), custom_call_target="tpu_custom_call" | custom-call | tf_op jit(solution)/shard_map/coarse/pallas_call | solution.py:529
  16.0 1.1 %stencil.1 = f32[9,16,2048]{2,1,0:T(8,128)} custom-call(f32[17,20,24,128]{3,2,1,0:T(8,128)S(1)} %get-tuple-element.8.fields, f32[9,16,2048]{2,1,0:T(8,128)S(1)} %get-tuple-element.9.held, f32[7,24,128]{2,1,0:T(8,128)S(1)} %get-tuple-element.10.carried), custom_call_target="tpu_custom_call" | custom-call | tf_op jit(solution)/shard_map/stencil/pallas_call | solution.py:558
